TPU v7x, 32 devices: a whole 2x2x4 slice. The times are simulated.
32 devices in a mesh: dp: 8 (over z, core), expert: 4 (over y, x).
Axes of the slice: x: 2, y: 2, z: 4, core: 2. Of those that a mesh axis runs over, the one named last changes fastest.
Arguments:
- tokens: bfloat16 [24576, 2048], P(('dp', 'expert')), may hold values from -6 to 6
- target: bfloat16 [24576, 2048], P(('dp', 'expert')), may hold values from -4 to 4
- route_index: int32 [8, 4, 4, 16], P('dp', None, 'expert'), may hold values from 0 to 767, as said below
- route_count: int32 [8, 4, 4], P('dp', None, 'expert'), may hold values from 1 to 16, as said below
- route_gate: float32 [8, 4, 4, 16], P('dp', None, 'expert'), may hold values from 0.1 to 1
- gate_weight: bfloat16 [2048, 4, 768], P('dp', 'expert'), may hold values from -0.125 to 0.125
- up_weight: bfloat16 [2048, 4, 768], P('dp', 'expert'), may hold values from -0.125 to 0.125
- down_weight: bfloat16 [2048, 4, 768], P('dp', 'expert'), may hold values from -0.21875 to 0.21875
Outputs:
- token_grad: bfloat16 [24576, 2048], P(('dp', 'expert'))
- gate_gradient: float32 [2048, 4, 768], P('dp', 'expert')
- up_gradient: float32 [2048, 4, 768], P('dp', 'expert')
- down_gradient: float32 [2048, 4, 768], P('dp', 'expert')
Inputs may be any that keep to these rules, and one draw needn't show every extreme that they name: `route_index`: within each list of 16 slots the indices are distinct; each names a token of the source device. `route_count`: in every group one expert has all 16 slots live from every source device; slots at or beyond the count are unused.
All inputs are finite; a program needn't handle non-finite values.
Results may differ from a plain program's by a relative error of at most 0.0059.
Values may be sent and summed in bfloat16 or wider, within the bound.
A program may use at most 128 MiB of HBM per device.

v0:
```python
import functools

import jax
import jax.numpy as jnp
from jax import lax
from jax.experimental import pallas as pl
from jax.experimental.pallas import tpu as pltpu
from jax.sharding import PartitionSpec as P

F32 = jnp.float32
BF16 = jnp.bfloat16
VMEM_LIMIT = 67000000
CORES = 2


def dot(a, b, dims, precision=None):
    return lax.dot_general(
        a, b, (dims, ((), ())), preferred_element_type=F32, precision=precision
    )


NN = ((1,), (0,))
NT = ((1,), (1,))
TN = ((0,), (0,))


def kernel(
    planes, experts, slots, factor,
    index, count, gate, tokens, target, gw, uw, dw,
    cb_out, hot_out, gg_out, ug_out, dg_out,
    TOK, TGT, ROWS, TROWS, W, R, EO, RET, SG, G, RG, CB, PS, PR, H, GU, RX, GX, HX, GUX,
    t_loc, g_loc, w_loc, w_send, w_recv, a_loc, a_send, a_recv, p_send, p_recv,
    h_send, h_recv, x_send, x_recv, GRADS, o_loc,
):
    dp = lax.axis_index("dp")
    me_e = lax.axis_index("expert")
    me_z = dp // CORES
    core = dp % CORES
    peers = planes * experts
    per_group = experts * slots
    half = gw.shape[0]
    chunk = CORES * half
    ff = gw.shape[1]
    me = me_z * experts + me_e
    sibling = {"dp": me_z * CORES + (1 - core), "expert": me_e}
    order = sorted(range(1, planes), key=lambda k: -min(k, planes - k))

    def at(z, e):
        return {"dp": z * CORES + core, "expert": e}

    def plane(k):
        return (me_z + k) % planes

    def slot_rows(n):
        return pl.ds(pl.multiple_of(n * slots, slots), slots)

    def cols(z):
        return pl.ds(pl.multiple_of(z * chunk, chunk), chunk)

    def group_rows(z):
        return pl.ds(pl.multiple_of(z * per_group, per_group), per_group)

    barrier = pltpu.get_barrier_semaphore()

    def greet(k, carry):
        p = (me + k) % peers
        pl.semaphore_signal(
            barrier, inc=1, device_id=at(p // experts, p % experts),
            device_id_type=pl.DeviceIdType.MESH,
        )
        return carry

    lax.fori_loop(1, peers, greet, 0)
    pl.semaphore_signal(
        barrier, inc=1, device_id=sibling, device_id_type=pl.DeviceIdType.MESH
    )
    tok_copies = {}
    for k in order + [0]:
        z = plane(k)
        tok_copies[k] = pltpu.make_async_copy(
            tokens.at[:, cols(z)], TOK.at[:, cols(z)], t_loc.at[k]
        )
        tok_copies[k].start()
    locals_w = []
    for i, w in enumerate((gw, uw, dw)):
        c = pltpu.make_async_copy(w, W.at[i, core], w_loc.at[i])
        c.start()
        locals_w.append(c)
    tgt_copy = pltpu.make_async_copy(target, TGT, g_loc)
    tgt_copy.start()

    lane = lax.broadcasted_iota(jnp.int32, (slots, slots), 1)
    own_lane = lane == lax.broadcasted_iota(jnp.int32, (slots, slots), 0)
    slot_id = lax.broadcasted_iota(jnp.int32, (slots, 1), 0)
    names, weights = [], []
    for e in range(experts):
        live = slot_id < jnp.broadcast_to(count[0:1, e : e + 1], (slots, 1))
        ids = jnp.broadcast_to(index[0, e], (slots, slots))
        ids = jnp.sum(jnp.where(own_lane, ids, 0), axis=1, keepdims=True)
        names.append(jnp.where(live, ids, -1))
        g = jnp.broadcast_to(gate[0, e], (slots, slots))
        g = jnp.sum(jnp.where(own_lane, g, 0.0), axis=1, keepdims=True)
        weights.append(jnp.where(live, g, 0.0))
    names = jnp.concatenate(names, axis=0)
    wcol = jnp.concatenate(weights, axis=0)
    hot = (
        names == lax.broadcasted_iota(jnp.int32, (per_group, TOK.shape[0]), 1)
    ).astype(F32).astype(BF16)
    hot_out[...] = hot

    def remote(src, dst, s, r, dev):
        c = pltpu.make_async_remote_copy(
            src_ref=src, dst_ref=dst, send_sem=s, recv_sem=r,
            device_id=dev, device_id_type=pl.DeviceIdType.MESH,
        )
        c.start()
        return c

    def to_plane(i, z, source, land):
        here = z == me_z

        @pl.when(here)
        def _():
            pltpu.make_async_copy(source(me_z, me_e), land, a_loc.at[i]).start()

        first = jnp.where(here, 1, 0)

        def send(j, carry):
            e = (me_e + j) % experts
            remote(source(z, e), land, a_send.at[i], a_recv.at[i, me_z], at(z, e))
            return carry

        lax.fori_loop(first, experts, send, 0)

    def owners(src, dst, i, z):
        to_plane(i, z, lambda z, e: src.at[slot_rows(e), cols(z)], dst.at[slot_rows(me)])

    def sources(src, dst, i, z):
        to_plane(
            i, z, lambda z, e: src.at[slot_rows(z * experts + e)],
            dst.at[slot_rows(me_e), cols(me_z)],
        )

    def take(sem, ref):
        pltpu.make_async_copy(ref, ref, sem).wait()

    def arrived(i, k):
        if k == 0:
            take(a_recv.at[i, me_z], R.at[pl.ds(0, (experts - 1) * slots)])
            take(a_loc.at[i], R.at[pl.ds(0, slots)])
        else:
            take(a_recv.at[i, plane(k)], R.at[pl.ds(0, per_group)])

    outs = []

    def put(i, src, dst):
        c = pltpu.make_async_copy(src, dst, o_loc.at[i])
        c.start()
        outs.append(c)

    def weight(i):
        return W[i].reshape(chunk, ff)

    pl.semaphore_wait(barrier, peers)
    for k in order + [0]:
        z = plane(k)
        tok_copies[k].wait()
        ROWS[:, cols(z)] = dot(hot, TOK[:, cols(z)], NN).astype(BF16)
        owners(ROWS, R, 0, z)
    sent_w = [
        remote(w, W.at[i, core], w_send.at[i], w_recv.at[i], sibling)
        for i, w in enumerate((gw, uw, dw))
    ]

    def send_sum(i, k):
        remote(
            PS.at[i, group_rows(plane(k))], PR.at[i, k - 1],
            p_send.at[i], p_recv.at[i, k - 1], at(plane(k), me_e),
        )

    def pass_on(buf, i, s, way):
        to = me_z + way

        @pl.when(jnp.logical_and(to >= 0, to < planes))
        def _():
            rows_s = buf.at[group_rows(s)]
            remote(
                rows_s, rows_s, h_send.at[i, (way + 1) // 2, s], h_recv.at[i, s],
                at(to, me_e),
            )

    def spread(buf, i):
        for way in (1, -1):
            pass_on(buf, i, me_z, way)

    def along(bufs, first, fn):
        fn(me_z)
        for far in range(1, planes):
            for way in (1, -1):
                s = me_z - way * far

                @pl.when(jnp.logical_and(s >= 0, s < planes))
                def _():
                    for j, buf in enumerate(bufs):
                        take(h_recv.at[first + j, s], buf.at[group_rows(s)])
                        pass_on(buf, first + j, s, way)
                    fn(s)

    def spread_sent(buf, i):
        for s in range(planes):
            rows_s = buf.at[pl.ds(s * per_group, per_group)]

            @pl.when(jnp.logical_and(me_z > 0, me_z <= s))
            def _():
                take(h_send.at[i, 0, s], rows_s)

            @pl.when(jnp.logical_and(me_z < planes - 1, me_z >= s))
            def _():
                take(h_send.at[i, 1, s], rows_s)

    def total(i, own):
        for k in order:
            take(p_recv.at[i, k - 1], PR.at[i, k - 1])
            own = own + PR[i, k - 1].astype(F32)
        return own

    keep = pl.ds(pl.multiple_of(core * half, half), half)
    give = pl.ds(pl.multiple_of((1 - core) * half, half), half)
    mine = group_rows(me_z)

    for i in range(2):
        locals_w[i].wait()
        sent_w[i].wait_recv()
    for k in order:
        z = plane(k)
        arrived(0, k)
        for i in range(2):
            PS[i, group_rows(z), :] = dot(R[group_rows(z), :], weight(i), NN).astype(BF16)
            send_sum(i, k)
    arrived(0, 0)
    gate_own = dot(R[mine, :], weight(0), NN)
    up_own = dot(R[mine, :], weight(1), NN)
    x_rows = remote(R.at[:, give], RX, x_send.at[0], x_recv.at[0], sibling)
    tgt_copy.wait()
    for z in range(planes):
        piece = slice(z * chunk, (z + 1) * chunk)
        TROWS[:, piece] = dot(hot, TGT[:, piece], NN)
    same = dot(hot, hot, NT).astype(BF16)
    gate_pre = total(0, gate_own)
    up_pre = total(1, up_own)
    sigma = jax.nn.sigmoid(gate_pre)
    active = gate_pre * sigma
    H[mine, :] = (active * up_pre).astype(BF16)
    spread(H, 0)
    locals_w[2].wait()
    sent_w[2].wait_recv()

    def expert_out(z):
        EO[group_rows(z), :] = dot(H[group_rows(z), :], weight(2), NT).astype(BF16)
        sources(EO, RET, 1, z)

    along([H], 0, expert_out)
    x_hidden = remote(H, HX, x_send.at[1], x_recv.at[1], sibling)
    for k in order + [0]:
        z = plane(k)
        arrived(1, k)
        part = wcol * RET[:, cols(z)].astype(F32)
        combined = -TROWS[:, cols(z)]
        for _ in range(3):
            top = part.astype(BF16)
            combined = combined + dot(same, top, NN)
            part = part - top.astype(F32)
        SG[:, cols(z)] = (wcol * combined).astype(BF16)
        owners(SG, G, 2, z)

    for k in order:
        z = plane(k)
        arrived(2, k)
        PS[2, group_rows(z), :] = dot(G[group_rows(z), :], weight(2), NN).astype(BF16)
        send_sum(2, k)
    arrived(2, 0)
    own = dot(G[mine, :], weight(2), NN)
    x_grad = remote(G.at[:, give], GX, x_send.at[2], x_recv.at[2], sibling)
    x_hidden.wait_recv()
    x_grad.wait_recv()
    GRADS[2] = (dot(G[:, keep], H[...], TN) + dot(GX[...], HX[...], TN)) * factor
    put(2, GRADS.at[2], dg_out)
    hidden_grad = total(2, own)
    GU[0, mine, :] = (
        hidden_grad * up_pre * sigma * (1.0 + gate_pre * (1.0 - sigma))
    ).astype(BF16)
    spread(GU.at[0], 1)
    GU[1, mine, :] = (hidden_grad * active).astype(BF16)
    spread(GU.at[1], 2)

    def row_grad(z):
        RG[group_rows(z), :] = (
            dot(GU[0, group_rows(z), :], weight(0), NT)
            + dot(GU[1, group_rows(z), :], weight(1), NT)
        ).astype(BF16)
        sources(RG, CB, 3, z)

    along([GU.at[0], GU.at[1]], 1, row_grad)
    x_gate = remote(GU.at[0], GUX.at[0], x_send.at[3], x_recv.at[3], sibling)
    x_up = remote(GU.at[1], GUX.at[1], x_send.at[4], x_recv.at[4], sibling)
    x_rows.wait_recv()
    x_gate.wait_recv()
    GRADS[0] = (dot(R[:, keep], GU[0], TN) + dot(RX[...], GUX[0], TN)) * factor
    put(0, GRADS.at[0], gg_out)
    x_up.wait_recv()
    GRADS[1] = (dot(R[:, keep], GU[1], TN) + dot(RX[...], GUX[1], TN)) * factor
    put(1, GRADS.at[1], ug_out)
    for k in order + [0]:
        arrived(3, k)
    put(3, CB, cb_out)

    for c in sent_w + [x_rows, x_hidden, x_grad, x_gate, x_up]:
        c.wait_send()
    for i in range(4):
        take(a_send.at[i], R.at[pl.ds(0, (peers - 1) * slots)])
    for i in range(3):
        take(p_send.at[i], PR.at[i])
    for i, buf in enumerate((H, GU.at[0], GU.at[1])):
        spread_sent(buf, i)
    for c in outs:
        c.wait()


def finish(hot, cb, gg, ug, dg, tg_out, gg_out, ug_out, dg_out):
    tg_out[...] = dot(hot[...], cb[...], TN).astype(BF16)
    gg_out[:, 0, :] = gg[...]
    ug_out[:, 0, :] = ug[...]
    dg_out[:, 0, :] = dg[...]


def on_device(
    tokens, target, route_index, route_count, route_gate, gate_weight, up_weight, down_weight
):
    groups = lax.axis_size("dp")
    experts = lax.axis_size("expert")
    planes = groups // CORES
    slots = route_index.shape[3]
    count, width = tokens.shape
    half, _, ff = gate_weight.shape
    chunk = CORES * half
    picked = experts * slots
    all_rows = planes * picked
    vmem = pl.BlockSpec(memory_space=pltpu.VMEM)
    anyw = pl.BlockSpec(memory_space=pl.ANY)
    dma = pltpu.SemaphoreType.DMA
    grad = jax.ShapeDtypeStruct((half, ff), F32)
    came_back, hot, gate_gradient, up_gradient, down_gradient = pl.pallas_call(
        functools.partial(
            kernel, planes, experts, slots, (groups * experts * slots) ** (-0.5)
        ),
        out_shape=(
            jax.ShapeDtypeStruct((picked, width), BF16),
            jax.ShapeDtypeStruct((picked, count), BF16),
            grad, grad, grad,
        ),
        in_specs=[vmem] * 3 + [anyw] * 5,
        out_specs=(anyw, vmem) + (anyw,) * 3,
        scratch_shapes=[
            pltpu.VMEM((count, width), BF16),
            pltpu.VMEM((count, width), BF16),
            pltpu.VMEM((picked, width), BF16),
            pltpu.VMEM((picked, width), F32),
            pltpu.VMEM((3, CORES, half, ff), BF16),
            pltpu.VMEM((all_rows, chunk), BF16),
            pltpu.VMEM((all_rows, chunk), BF16),
            pltpu.VMEM((picked, width), BF16),
            pltpu.VMEM((picked, width), BF16),
            pltpu.VMEM((all_rows, chunk), BF16),
            pltpu.VMEM((all_rows, chunk), BF16),
            pltpu.VMEM((picked, width), BF16),
            pltpu.VMEM((3, all_rows, ff), BF16),
            pltpu.VMEM((3, planes - 1, picked, ff), BF16),
            pltpu.VMEM((all_rows, ff), BF16),
            pltpu.VMEM((2, all_rows, ff), BF16),
            pltpu.VMEM((all_rows, half), BF16),
            pltpu.VMEM((all_rows, half), BF16),
            pltpu.VMEM((all_rows, ff), BF16),
            pltpu.VMEM((2, all_rows, ff), BF16),
            dma((planes,)), dma,
            dma((3,)), dma((3,)), dma((3,)),
            dma((4,)), dma((4,)), dma((4, planes)),
            dma((3,)), dma((3, planes)),
            dma((3, 2, planes)), dma((3, planes)),
            dma((5,)), dma((5,)),
            pltpu.VMEM((3, half, ff), F32), dma((4,)),
        ],
        compiler_params=pltpu.CompilerParams(
            collective_id=0, has_side_effects=True, vmem_limit_bytes=VMEM_LIMIT
        ),
        name="routed_layer",
    )(
        route_index, route_count.reshape(1, experts), route_gate, tokens, target,
        gate_weight.reshape(half, ff), up_weight.reshape(half, ff),
        down_weight.reshape(half, ff),
    )
    steps = 2
    part = pl.BlockSpec((half // steps, ff), lambda i: (i, 0))
    part_out = pl.BlockSpec((half // steps, 1, ff), lambda i: (i, 0, 0))
    grad = jax.ShapeDtypeStruct((half, 1, ff), F32)
    return tuple(pl.pallas_call(
        finish,
        grid=(steps,),
        out_shape=(jax.ShapeDtypeStruct((count, width), BF16), grad, grad, grad),
        in_specs=[
            pl.BlockSpec((picked, count // steps), lambda i: (0, i)),
            pl.BlockSpec((picked, width), lambda i: (0, 0)),
            part, part, part,
        ],
        out_specs=(
            pl.BlockSpec((count // steps, width), lambda i: (i, 0)),
            part_out, part_out, part_out,
        ),
        compiler_params=pltpu.CompilerParams(vmem_limit_bytes=VMEM_LIMIT),
        name="finish",
    )(hot, came_back, gate_gradient, up_gradient, down_gradient))


def solution(mesh):
    return jax.shard_map(
        on_device,
        mesh=mesh,
        in_specs=(
            P(("dp", "expert"), None),
            P(("dp", "expert"), None),
            P("dp", None, "expert", None),
            P("dp", None, "expert"),
            P("dp", None, "expert", None),
            P("dp", "expert", None),
            P("dp", "expert", None),
            P("dp", "expert", None),
        ),
        out_specs=(
            P(("dp", "expert"), None),
            P("dp", "expert", None),
            P("dp", "expert", None),
            P("dp", "expert", None),
        ),
        check_vma=False,
    )
```

profile of v0, /device:TPU:0, one launch (start us, length us, event | category | flops | bytes accessed | tf_op | source)
XLA Modules:
  0.0 90.0 jit_solution(5559549125590348299)
XLA Ops:
  0.6 84.8 %routed_layer.1 = (bf16[64,2048]{1,0:T(8,128)(2,1)}, bf16[64,768]{1,0:T(8,128)(2,1)}, f32[256,768]{1,0:T(8,128)}, f32[256,768]{1,0:T(8,128)}, f32[256,768]{1,0:T(8,128)}) custom-call(s32[1,4,1,16]{3,2,1,0:T(1,128)} %index.1, s32[1,4]{1,0:T(1,128)} %bitcast.7, f32[1,4,1,16]{3,2,1,0:T(1,128)} %gate.1, bf16[768,2048]{1,0:T(8,128)(2,1)} %tokens.1, ...), custom_call_target="tpu_custom_call" | custom-call | tf_op jit(solution)/shard_map/routed_layer/pallas_call | solution.py:352
  85.4 4.5 %finish.1 = (bf16[768,2048]{1,0:T(8,128)(2,1)}, f32[256,1,768]{2,1,0:T(1,128)}, f32[256,1,768]{2,1,0:T(1,128)}, f32[256,1,768]{2,1,0:T(1,128)}) custom-call(bf16[64,768]{1,0:T(8,128)(2,1)} %get-tuple-element.9.hot, bf16[64,2048]{1,0:T(8,128)(2,1)} %get-tuple-element.10.cb, f32[256,768]{1,0:T(8,128)} %get-tuple-element.11.gg, ...), custom_call_target="tpu_custom_call" | custom-call | tf_op jit(solution)/shard_map/finish/pallas_call | solution.py:405
where the time goes:
time: 90.1 us; the launch traced here: 90 us
  Pallas kernels  89.3 us (99%)
    pallas_call x1, Pallas kernels, on_device(): pl.pallas_call(functools.partial(kernel, planes, experts, slots, (groups...  84.8 us
    pallas_call x1, Pallas kernels, on_device(): pl.pallas_call(finish, grid=(steps,), out_shape=(jax.ShapeDtypeStruct((co...  4.52 us

commit v1 on v0

--- a/solution.py
+++ b/solution.py
@@ -1,4 +1,6 @@
+import contextlib
 import functools
+import math
 
 import jax
 import jax.numpy as jnp
@@ -11,6 +13,10 @@
 BF16 = jnp.bfloat16
 VMEM_LIMIT = 67000000
 CORES = 2
+PIECES = 3
+LAG = 2
+LAG_PLANE = 2
+LAG_BACK = 2
 
 
 def dot(a, b, dims, precision=None):
@@ -19,12 +25,16 @@
     )
 
 
+def scope(name):
+    return contextlib.nullcontext()
+
+
 NN = ((1,), (0,))
 NT = ((1,), (1,))
 TN = ((0,), (0,))
 
 
-def kernel(
+def direct_kernel(
     planes, experts, slots, factor,
     index, count, gate, tokens, target, gw, uw, dw,
     cb_out, hot_out, gg_out, ug_out, dg_out,
@@ -326,11 +336,455 @@
         c.wait()
 
 
+def chain_kernel(
+    planes, experts, slots, factor, pieces,
+    index, count, gate, tokens, target, gw, uw, dw,
+    cb_out, hot_out, gg_out, ug_out, dg_out,
+    TOK, TGT, ROWS, TROWS, META, MT, W, R, TR, G, EOG,
+    OWN, IN, OUT, HOWN, HIN, HOUT, H, GU, RG, CB, RX, GX, HX, GUX, GRADS,
+    t_loc, g_loc, w_loc, w_send, w_recv, a_send, a_recv, e_send, e_recv,
+    c_send, c_recv, h_send, h_recv, x_send, x_recv, o_loc,
+):
+    dp = lax.axis_index("dp")
+    me_e = lax.axis_index("expert")
+    me_z = dp // CORES
+    core = dp % CORES
+    peers = planes * experts
+    per_group = experts * slots
+    half = gw.shape[0]
+    chunk = CORES * half
+    ff = gw.shape[1]
+    fw = ff // pieces
+    me = me_z * experts + me_e
+    sibling = {"dp": me_z * CORES + (1 - core), "expert": me_e}
+    far_first = sorted(range(1, planes), key=lambda k: -min(k, planes - k)) + [0]
+    ways = (1, -1)
+    dist = (me_z, planes - 1 - me_z)
+    depth = jnp.maximum(dist[0], dist[1])
+
+    def at(z, e):
+        return {"dp": z * CORES + core, "expert": e}
+
+    def plane(k):
+        return (me_z + k) % planes
+
+    def slot_rows(n):
+        return pl.ds(pl.multiple_of(n * slots, slots), slots)
+
+    def cols(z):
+        return pl.ds(pl.multiple_of(z * chunk, chunk), chunk)
+
+    def group_rows(z):
+        return pl.ds(pl.multiple_of(z * per_group, per_group), per_group)
+
+    def turn(g):
+        if planes % 2:
+            return g
+        return planes // 2 - 1 - g // 2 + (g % 2) * (2 * (g // 2) + 1)
+
+    barrier = pltpu.get_barrier_semaphore()
+
+    def greet(k, carry):
+        p = (me + k) % peers
+        pl.semaphore_signal(
+            barrier, inc=1, device_id=at(p // experts, p % experts),
+            device_id_type=pl.DeviceIdType.MESH,
+        )
+        return carry
+
+    lax.fori_loop(1, peers, greet, 0)
+    pl.semaphore_signal(
+        barrier, inc=1, device_id=sibling, device_id_type=pl.DeviceIdType.MESH
+    )
+    tok_copies = {}
+    for k in far_first:
+        tok_copies[k] = pltpu.make_async_copy(
+            tokens.at[:, cols(plane(k))], TOK.at[:, cols(plane(k))], t_loc.at[k]
+        )
+        tok_copies[k].start()
+    locals_w = []
+    keep = pl.ds(pl.multiple_of(core * half, half), half)
+    give = pl.ds(pl.multiple_of((1 - core) * half, half), half)
+    for i, w in enumerate((gw, uw, dw)):
+        c = pltpu.make_async_copy(w, W.at[i, keep], w_loc.at[i])
+        c.start()
+        locals_w.append(c)
+    tgt_copy = pltpu.make_async_copy(target, TGT, g_loc)
+    tgt_copy.start()
+
+    lane = lax.broadcasted_iota(jnp.int32, (slots, slots), 1)
+    own_lane = lane == lax.broadcasted_iota(jnp.int32, (slots, slots), 0)
+    slot_id = lax.broadcasted_iota(jnp.int32, (slots, 1), 0)
+    names, weights = [], []
+    for e in range(experts):
+        live = slot_id < jnp.broadcast_to(count[0:1, e : e + 1], (slots, 1))
+        ids = jnp.broadcast_to(index[0, e], (slots, slots))
+        ids = jnp.sum(jnp.where(own_lane, ids, 0), axis=1, keepdims=True)
+        names.append(jnp.where(live, ids, -1))
+        g = jnp.broadcast_to(gate[0, e], (slots, slots))
+        g = jnp.sum(jnp.where(own_lane, g, 0.0), axis=1, keepdims=True)
+        weights.append(jnp.where(live, g, 0.0))
+    names = jnp.concatenate(names, axis=0)
+    wcol = jnp.concatenate(weights, axis=0)
+    hot = (
+        names == lax.broadcasted_iota(jnp.int32, (per_group, TOK.shape[0]), 1)
+    ).astype(F32).astype(BF16)
+    hot_out[...] = hot
+
+    def remote(src, dst, s, r, dev):
+        c = pltpu.make_async_remote_copy(
+            src_ref=src, dst_ref=dst, send_sem=s, recv_sem=r,
+            device_id=dev, device_id_type=pl.DeviceIdType.MESH,
+        )
+        c.start()
+        return c
+
+    def take(sem, ref):
+        pltpu.make_async_copy(ref, ref, sem).wait()
+
+    def to_plane(i, z, source, land):
+        here = z == me_z
+
+        @pl.when(here)
+        def _():
+            pltpu.make_async_copy(source(me_z, me_e), land, a_recv.at[i, me_z]).start()
+
+        def send(j, carry):
+            e = (me_e + j) % experts
+            remote(source(z, e), land, a_send.at[i], a_recv.at[i, me_z], at(z, e))
+            return carry
+
+        lax.fori_loop(jnp.where(here, 1, 0), experts, send, 0)
+
+    for k in far_first:
+        z = plane(k)
+        tok_copies[k].wait()
+        ROWS[:, cols(z)] = dot(hot, TOK[:, cols(z)], NN).astype(BF16)
+    for way, d in zip(ways, range(2)):
+        @pl.when(dist[d] == 0)
+        def _():
+            IN[d] = jnp.zeros(IN.shape[1:], BF16)
+            HIN[d] = jnp.zeros(HIN.shape[1:], BF16)
+
+    with scope("barrier"):
+        pl.semaphore_wait(barrier, peers)
+    sent_w = [
+        remote(w, W.at[i, keep], w_send.at[i], w_recv.at[i], sibling)
+        for i, w in enumerate((gw, uw, dw))
+    ]
+    for k in far_first:
+        to_plane(
+            0, plane(k), lambda z, e: ROWS.at[slot_rows(e), cols(z)], R.at[slot_rows(me)]
+        )
+    with scope("trows"):
+        tgt_copy.wait()
+        for k in far_first:
+            z = plane(k)
+            TROWS[:, cols(z)] = dot(hot, TGT[:, cols(z)], NN).astype(BF16)
+            to_plane(
+                1, z, lambda z, e: TROWS.at[slot_rows(e), cols(z)], TR.at[slot_rows(me)]
+            )
+    with scope("meta"):
+        square = (per_group, per_group)
+        eye = lax.broadcasted_iota(jnp.int32, square, 0) == lax.broadcasted_iota(
+            jnp.int32, square, 1
+        )
+        wrow = jnp.sum(jnp.where(eye, wcol, 0.0), axis=0, keepdims=True)
+        mix = wcol * dot(hot, hot, NT) * wrow
+        pad = (META.shape[1] - 256) // 2
+        META[...] = jnp.zeros(META.shape, BF16)
+        for part, start, stop in (
+            (mix, 0, per_group), (jnp.broadcast_to(wcol, (per_group, 128)), 2 * pad, 2 * pad + 128)
+        ):
+            top = part.astype(BF16)
+            step = pad if start == 0 else 128
+            META[:, start:stop] = top
+            META[:, start + step : stop + step] = (part - top.astype(F32)).astype(BF16)
+        for k in far_first:
+            to_plane(2, plane(k), lambda z, e: META.at[slot_rows(e)], MT.at[slot_rows(me)])
+
+    with scope("w_wait"):
+        for i in range(3):
+            locals_w[i].wait()
+            sent_w[i].wait_recv()
+
+    def piece(f):
+        return pl.ds(pl.multiple_of(f * fw, fw), fw)
+
+    def group_of(c):
+        return turn(c // pieces)
+
+    def rows_in(z):
+        take(a_recv.at[0, z], R.at[pl.ds(0, per_group)])
+
+    def partial_sums(c):
+        z, f = group_of(c), c % pieces
+
+        @pl.when(f == 0)
+        def _():
+            with scope("x_wait"):
+                rows_in(z)
+
+        with scope("own"):
+            rows = R[group_rows(z), :]
+            for i in range(2):
+                OWN[c, :, i * fw : (i + 1) * fw] = dot(rows, W[i, :, piece(f)], NN)
+
+    def move(own, inn, out, send, recv, d, c):
+        @pl.when(dist[d] > 0)
+        def _():
+            with scope("mv%d" % (own is HOWN)):
+                take(recv.at[d, c], inn.at[d, c])
+
+        @pl.when(dist[d] < planes - 1)
+        def _():
+            out[d, c] = (own[c] + inn[d, c].astype(F32)).astype(BF16)
+            remote(
+                out.at[d, c], inn.at[d, c], send.at[d], recv.at[d, c],
+                at(me_z + ways[d], me_e),
+            )
+
+    def total(own, inn, c):
+        return own[c] + inn[0, c].astype(F32) + inn[1, c].astype(F32)
+
+    def to_sibling(i, src, dst):
+        remote(src, dst, x_send.at[i], x_recv.at[i], sibling)
+
+    def forward(c):
+        z, f = group_of(c), c % pieces
+        with scope("fwd"):
+            both = total(OWN, IN, c)
+            OWN[c] = both
+            pre, up = both[:, :fw], both[:, fw:]
+            H[group_rows(z), piece(f)] = (pre * jax.nn.sigmoid(pre) * up).astype(BF16)
+
+        @pl.when(f == pieces - 1)
+        def _():
+            with scope("eo"):
+                EOG[z, me_e] = dot(H[group_rows(z), :], W[2], NT).astype(BF16)
+
+                def send(j, carry):
+                    remote(
+                        EOG.at[z, me_e], EOG.at[z, me_e], e_send, e_recv.at[z],
+                        at(me_z, (me_e + j) % experts),
+                    )
+                    return carry
+
+                lax.fori_loop(1, experts, send, 0)
+                to_sibling(1, H.at[group_rows(z)], HX.at[group_rows(z)])
+
+    def slot_grads(g):
+        z = turn(g)
+        with scope("eo_wait"):
+            take(e_recv.at[z], EOG.at[z, pl.ds(0, experts - 1)])
+            take(a_recv.at[1, z], TR.at[pl.ds(0, per_group)])
+            take(a_recv.at[2, z], MT.at[pl.ds(0, per_group)])
+        with scope("comb"):
+            for s in range(experts):
+                its = slice(s * slots, (s + 1) * slots)
+                mine = slot_rows(z * experts + s)
+                outs = jnp.concatenate([EOG[z, e, its, :] for e in range(experts)], axis=0)
+                wide = dot(MT[mine, 0:per_group], outs, NN) + dot(
+                    MT[mine, pad : pad + per_group], outs, NN
+                )
+                w = MT[mine, 2 * pad : 2 * pad + 1].astype(F32) + MT[
+                    mine, 2 * pad + 128 : 2 * pad + 129
+                ].astype(F32)
+                G[mine, :] = (wide - w * TR[mine, :].astype(F32)).astype(BF16)
+            HOWN[g] = dot(G[group_rows(z), :], W[2], NN)
+            to_sibling(2, G.at[group_rows(z), give], GX.at[group_rows(z)])
+
+    def backward(g):
+        z = turn(g)
+        rows = group_rows(z)
+        with scope("bwd"):
+            hidden_grad = total(HOWN, HIN, g)
+            for f in range(pieces):
+                both = OWN[g * pieces + f]
+                pre, up = both[:, :fw], both[:, fw:]
+                grad = hidden_grad[:, f * fw : (f + 1) * fw]
+                sigma = jax.nn.sigmoid(pre)
+                GU[0, rows, f * fw : (f + 1) * fw] = (
+                    grad * up * sigma * (1.0 + pre * (1.0 - sigma))
+                ).astype(BF16)
+                GU[1, rows, f * fw : (f + 1) * fw] = (grad * (pre * sigma)).astype(BF16)
+            RG[rows, :] = (
+                dot(GU[0, rows, :], W[0], NT) + dot(GU[1, rows, :], W[1], NT)
+            ).astype(BF16)
+            to_plane(
+                3, z, lambda z, e: RG.at[slot_rows(z * experts + e)],
+                CB.at[slot_rows(me_e), cols(me_z)],
+            )
+            for i in range(2):
+                to_sibling(3 + i, GU.at[i, rows], GUX.at[i, rows])
+
+    steps = planes * pieces
+    ready = LAG * depth
+    combined = pieces - 1 + ready + LAG_PLANE
+    started = pieces - 1 + LAG * (planes - 1) + LAG_PLANE
+    moved = started + LAG_BACK * depth
+
+    def each(t, fn, last):
+        @pl.when(jnp.logical_and(t >= 0, t < last))
+        def _():
+            fn(t)
+
+    def each_group(t, fn):
+        @pl.when(jnp.logical_and(jnp.logical_and(t >= 0, t < steps), t % pieces == 0))
+        def _():
+            fn(t // pieces)
+
+    def grad(i, left, left_x, right, right_x, out):
+        GRADS[i] = (dot(left, right, TN) + dot(left_x, right_x, TN)) * factor
+        c = pltpu.make_async_copy(GRADS.at[i], out, o_loc.at[i])
+        c.start()
+
+    def tick(t, carry):
+        each(t, partial_sums, steps)
+        for d in range(2):
+            each(
+                t - LAG * dist[d],
+                functools.partial(move, OWN, IN, OUT, c_send, c_recv, d), steps,
+            )
+        each(t - ready, forward, steps)
+        each_group(t - combined, slot_grads)
+        for d in range(2):
+            each_group(
+                t - started - LAG_BACK * dist[d],
+                functools.partial(move, HOWN, HIN, HOUT, h_send, h_recv, d),
+            )
+        each_group(t - moved, backward)
+        return carry
+
+    end = steps - pieces + pieces - 1 + (LAG + LAG_BACK) * (planes - 1) + LAG_PLANE + 1
+    middle = steps - pieces + pieces - 1 + LAG * (planes - 1) + LAG_PLANE + 1
+    lax.fori_loop(0, middle, tick, 0)
+    to_sibling(0, R.at[:, give], RX)
+    with scope("dgrad"):
+        take(x_recv.at[1], HX)
+        take(x_recv.at[2], GX)
+        grad(2, G[:, keep], GX[...], H[...], HX[...], dg_out)
+    lax.fori_loop(middle, end, tick, 0)
+    with scope("xg"):
+        take(x_recv.at[0], RX)
+        take(x_recv.at[3], GUX.at[0])
+        take(x_recv.at[4], GUX.at[1])
+    with scope("gugrad"):
+        grad(0, R[:, keep], RX[...], GU[0], GUX[0], gg_out)
+        grad(1, R[:, keep], RX[...], GU[1], GUX[1], ug_out)
+    with scope("cb_wait"):
+        for k in far_first:
+            take(a_recv.at[3, plane(k)], R.at[pl.ds(0, per_group)])
+    with scope("tail"):
+        back = pltpu.make_async_copy(CB, cb_out, o_loc.at[3])
+        back.start()
+        for c in sent_w:
+            c.wait_send()
+        others = pl.ds(0, (peers - 1) * slots)
+        for i, buf in enumerate((R, TR, MT, RG)):
+            take(a_send.at[i], buf.at[others])
+        take(e_send, EOG.at[:, pl.ds(0, experts - 1)])
+        for d in range(2):
+            @pl.when(dist[d] < planes - 1)
+            def _():
+                take(c_send.at[d], OUT.at[d])
+                take(h_send.at[d], HOUT.at[d])
+        for i, buf in enumerate((RX, HX, GX, GUX.at[0], GUX.at[1])):
+            take(x_send.at[i], buf)
+        for i, out in enumerate((gg_out, ug_out, dg_out)):
+            pltpu.make_async_copy(GRADS.at[i], out, o_loc.at[i]).wait()
+        back.wait()
+
+
 def finish(hot, cb, gg, ug, dg, tg_out, gg_out, ug_out, dg_out):
     tg_out[...] = dot(hot[...], cb[...], TN).astype(BF16)
     gg_out[:, 0, :] = gg[...]
     ug_out[:, 0, :] = ug[...]
     dg_out[:, 0, :] = dg[...]
+
+
+def direct_scratch(planes, picked, count, width, half, ff):
+    chunk = CORES * half
+    all_rows = planes * picked
+    dma = pltpu.SemaphoreType.DMA
+    return [
+        pltpu.VMEM((count, width), BF16),
+        pltpu.VMEM((count, width), BF16),
+        pltpu.VMEM((picked, width), BF16),
+        pltpu.VMEM((picked, width), F32),
+        pltpu.VMEM((3, CORES, half, ff), BF16),
+        pltpu.VMEM((all_rows, chunk), BF16),
+        pltpu.VMEM((all_rows, chunk), BF16),
+        pltpu.VMEM((picked, width), BF16),
+        pltpu.VMEM((picked, width), BF16),
+        pltpu.VMEM((all_rows, chunk), BF16),
+        pltpu.VMEM((all_rows, chunk), BF16),
+        pltpu.VMEM((picked, width), BF16),
+        pltpu.VMEM((3, all_rows, ff), BF16),
+        pltpu.VMEM((3, planes - 1, picked, ff), BF16),
+        pltpu.VMEM((all_rows, ff), BF16),
+        pltpu.VMEM((2, all_rows, ff), BF16),
+        pltpu.VMEM((all_rows, half), BF16),
+        pltpu.VMEM((all_rows, half), BF16),
+        pltpu.VMEM((all_rows, ff), BF16),
+        pltpu.VMEM((2, all_rows, ff), BF16),
+        dma((planes,)), dma,
+        dma((3,)), dma((3,)), dma((3,)),
+        dma((4,)), dma((4,)), dma((4, planes)),
+        dma((3,)), dma((3, planes)),
+        dma((3, 2, planes)), dma((3, planes)),
+        dma((5,)), dma((5,)),
+        pltpu.VMEM((3, half, ff), F32), dma((4,)),
+    ]
+
+
+def chain_scratch(planes, experts, picked, count, width, half, ff, pieces):
+    chunk = CORES * half
+    all_rows = planes * picked
+    steps = planes * pieces
+    fw = ff // pieces
+    table = 2 * (-(-picked // 128) * 128) + 256
+    dma = pltpu.SemaphoreType.DMA
+    return [
+        pltpu.VMEM((count, width), BF16),
+        pltpu.VMEM((count, width), BF16),
+        pltpu.VMEM((picked, width), BF16),
+        pltpu.VMEM((picked, width), BF16),
+        pltpu.VMEM((picked, table), BF16),
+        pltpu.VMEM((all_rows, table), BF16),
+        pltpu.VMEM((3, chunk, ff), BF16),
+        pltpu.VMEM((all_rows, chunk), BF16),
+        pltpu.VMEM((all_rows, chunk), BF16),
+        pltpu.VMEM((all_rows, chunk), BF16),
+        pltpu.VMEM((planes, experts, picked, chunk), BF16),
+        pltpu.VMEM((steps, picked, 2 * fw), F32),
+        pltpu.VMEM((2, steps, picked, 2 * fw), BF16),
+        pltpu.VMEM((2, steps, picked, 2 * fw), BF16),
+        pltpu.VMEM((planes, picked, ff), F32),
+        pltpu.VMEM((2, planes, picked, ff), BF16),
+        pltpu.VMEM((2, planes, picked, ff), BF16),
+        pltpu.VMEM((all_rows, ff), BF16),
+        pltpu.VMEM((2, all_rows, ff), BF16),
+        pltpu.VMEM((all_rows, chunk), BF16),
+        pltpu.VMEM((picked, width), BF16),
+        pltpu.VMEM((all_rows, half), BF16),
+        pltpu.VMEM((all_rows, half), BF16),
+        pltpu.VMEM((all_rows, ff), BF16),
+        pltpu.VMEM((2, all_rows, ff), BF16),
+        pltpu.VMEM((3, half, ff), F32),
+        dma((planes,)), dma, dma((3,)), dma((3,)), dma((3,)),
+        dma((4,)), dma((4, planes)), dma, dma((planes,)),
+        dma((2,)), dma((2, steps)), dma((2,)), dma((2, planes)),
+        dma((5,)), dma((5,)), dma((4,)),
+    ]
+
+
+def held_bytes(scratch):
+    return sum(
+        math.prod(s.shape) * jnp.dtype(s.dtype).itemsize
+        for s in scratch
+        if getattr(s, "memory_space", None) == pltpu.VMEM
+    )
 
 
 def on_device(
@@ -342,17 +796,19 @@
     slots = route_index.shape[3]
     count, width = tokens.shape
     half, _, ff = gate_weight.shape
-    chunk = CORES * half
     picked = experts * slots
-    all_rows = planes * picked
+    factor = (groups * experts * slots) ** (-0.5)
+    pieces = max(n for n in range(1, PIECES + 1) if ff % (128 * n) == 0)
     vmem = pl.BlockSpec(memory_space=pltpu.VMEM)
     anyw = pl.BlockSpec(memory_space=pl.ANY)
-    dma = pltpu.SemaphoreType.DMA
     grad = jax.ShapeDtypeStruct((half, ff), F32)
+    scratch = chain_scratch(planes, experts, picked, count, width, half, ff, pieces)
+    body = functools.partial(chain_kernel, planes, experts, slots, factor, pieces)
+    if held_bytes(scratch) > VMEM_LIMIT * 3 // 4:
+        scratch = direct_scratch(planes, picked, count, width, half, ff)
+        body = functools.partial(direct_kernel, planes, experts, slots, factor)
     came_back, hot, gate_gradient, up_gradient, down_gradient = pl.pallas_call(
-        functools.partial(
-            kernel, planes, experts, slots, (groups * experts * slots) ** (-0.5)
-        ),
+        body,
         out_shape=(
             jax.ShapeDtypeStruct((picked, width), BF16),
             jax.ShapeDtypeStruct((picked, count), BF16),
@@ -360,35 +816,7 @@
         ),
         in_specs=[vmem] * 3 + [anyw] * 5,
         out_specs=(anyw, vmem) + (anyw,) * 3,
-        scratch_shapes=[
-            pltpu.VMEM((count, width), BF16),
-            pltpu.VMEM((count, width), BF16),
-            pltpu.VMEM((picked, width), BF16),
-            pltpu.VMEM((picked, width), F32),
-            pltpu.VMEM((3, CORES, half, ff), BF16),
-            pltpu.VMEM((all_rows, chunk), BF16),
-            pltpu.VMEM((all_rows, chunk), BF16),
-            pltpu.VMEM((picked, width), BF16),
-            pltpu.VMEM((picked, width), BF16),
-            pltpu.VMEM((all_rows, chunk), BF16),
-            pltpu.VMEM((all_rows, chunk), BF16),
-            pltpu.VMEM((picked, width), BF16),
-            pltpu.VMEM((3, all_rows, ff), BF16),
-            pltpu.VMEM((3, planes - 1, picked, ff), BF16),
-            pltpu.VMEM((all_rows, ff), BF16),
-            pltpu.VMEM((2, all_rows, ff), BF16),
-            pltpu.VMEM((all_rows, half), BF16),
-            pltpu.VMEM((all_rows, half), BF16),
-            pltpu.VMEM((all_rows, ff), BF16),
-            pltpu.VMEM((2, all_rows, ff), BF16),
-            dma((planes,)), dma,
-            dma((3,)), dma((3,)), dma((3,)),
-            dma((4,)), dma((4,)), dma((4, planes)),
-            dma((3,)), dma((3, planes)),
-            dma((3, 2, planes)), dma((3, planes)),
-            dma((5,)), dma((5,)),
-            pltpu.VMEM((3, half, ff), F32), dma((4,)),
-        ],
+        scratch_shapes=scratch,
         compiler_params=pltpu.CompilerParams(
             collective_id=0, has_side_effects=True, vmem_limit_bytes=VMEM_LIMIT
         ),

time: 90.1 us -> 81.4 us (0.903)
  Pallas kernels: 89.3 us -> 80.1 us
    pallas_call x1, Pallas kernels: 84.8 us -> 75.5 us  [on_device(): pl.pallas_call(body, out_shape=(jax.ShapeDtypeStruct((picked, width), BF1...]
where the time goes in v1:
time: 81.4 us; the launch traced here: 80.7 us
  Pallas kernels  80.1 us (98%)
    pallas_call x1, Pallas kernels, on_device(): pl.pallas_call(body, out_shape=(jax.ShapeDtypeStruct((picked, width), BF1...  75.5 us
    pallas_call x1, Pallas kernels, on_device(): pl.pallas_call(finish, grid=(steps,), out_shape=(jax.ShapeDtypeStruct((co...  4.52 us

profile of v1, /device:TPU:0, one launch (start us, length us, event | category | flops | bytes accessed | tf_op | source)
XLA Modules:
  0.0 80.7 jit_solution(1988763229395186317)
XLA Ops:
  0.6 75.5 %routed_layer.1 = (bf16[64,2048]{1,0:T(8,128)(2,1)}, bf16[64,768]{1,0:T(8,128)(2,1)}, f32[256,768]{1,0:T(8,128)}, f32[256,768]{1,0:T(8,128)}, f32[256,768]{1,0:T(8,128)}) custom-call(s32[1,4,1,16]{3,2,1,0:T(1,128)} %index.1, s32[1,4]{1,0:T(1,128)} %bitcast.7, f32[1,4,1,16]{3,2,1,0:T(1,128)} %gate.1, bf16[768,2048]{1,0:T(8,128)(2,1)} %tokens.1, ...), custom_call_target="tpu_custom_call" | custom-call | tf_op jit(solution)/shard_map/routed_layer/pallas_call | solution.py:810
  76.2 4.5 %finish.1 = (bf16[768,2048]{1,0:T(8,128)(2,1)}, f32[256,1,768]{2,1,0:T(1,128)}, f32[256,1,768]{2,1,0:T(1,128)}, f32[256,1,768]{2,1,0:T(1,128)}) custom-call(bf16[64,768]{1,0:T(8,128)(2,1)} %get-tuple-element.9.hot, bf16[64,2048]{1,0:T(8,128)(2,1)} %get-tuple-element.10.cb, f32[256,768]{1,0:T(8,128)} %get-tuple-element.11.gg, ...), custom_call_target="tpu_custom_call" | custom-call | tf_op jit(solution)/shard_map/finish/pallas_call | solution.py:833

commit v2 on v1

--- a/solution.py
+++ b/solution.py
@@ -14,9 +14,17 @@
 VMEM_LIMIT = 67000000
 CORES = 2
 PIECES = 3
-LAG = 2
-LAG_PLANE = 2
-LAG_BACK = 2
+LAG = 3
+LAG_PLANE = 4
+LAG_BACK = 4
+LAG_ROWS = 0
+BACK_PIECES = 3
+TARGET_AT = -1
+TARGET_STEP = 0
+NEAR_TOKENS = False
+NEAR_TARGETS = False
+CHAIN_LIMIT = 44000000
+FINISH_LIMIT = 40000000
 
 
 def dot(a, b, dims, precision=None):
@@ -338,12 +346,12 @@
 
 def chain_kernel(
     planes, experts, slots, factor, pieces,
-    index, count, gate, tokens, target, gw, uw, dw,
+    index_in, count_in, gate_in, tokens, target, gw, uw, dw,
     cb_out, hot_out, gg_out, ug_out, dg_out,
-    TOK, TGT, ROWS, TROWS, META, MT, W, R, TR, G, EOG,
-    OWN, IN, OUT, HOWN, HIN, HOUT, H, GU, RG, CB, RX, GX, HX, GUX, GRADS,
+    index, count, gate, r_loc, TOK, TGT, ROWS, TROWS, META, MT, W, R, TR, G, EOG,
+    OWN, IN, OUT, HOWN, HIN, HOUT, H, GU, RG, CB, RX, GX, HX, GUX,
     t_loc, g_loc, w_loc, w_send, w_recv, a_send, a_recv, e_send, e_recv,
-    c_send, c_recv, h_send, h_recv, x_send, x_recv, o_loc,
+    c_send, c_recv, h_send, h_recv, x_send, x_recv,
 ):
     dp = lax.axis_index("dp")
     me_e = lax.axis_index("expert")
@@ -355,10 +363,14 @@
     chunk = CORES * half
     ff = gw.shape[1]
     fw = ff // pieces
+    split = HIN.shape[1] // planes
+    hw = ff // split
     me = me_z * experts + me_e
     sibling = {"dp": me_z * CORES + (1 - core), "expert": me_e}
-    far_first = sorted(range(1, planes), key=lambda k: -min(k, planes - k)) + [0]
     ways = (1, -1)
+    side = jnp.where(2 * me_z < planes, 1, -1)
+    near_first = list(range(1, planes)) + [0]
+    far_first = sorted(range(1, planes), key=lambda k: abs(k - planes / 2)) + [0]
     dist = (me_z, planes - 1 - me_z)
     depth = jnp.maximum(dist[0], dist[1])
 
@@ -366,7 +378,7 @@
         return {"dp": z * CORES + core, "expert": e}
 
     def plane(k):
-        return (me_z + k) % planes
+        return (me_z + side * k + planes) % planes
 
     def slot_rows(n):
         return pl.ds(pl.multiple_of(n * slots, slots), slots)
@@ -396,6 +408,14 @@
     pl.semaphore_signal(
         barrier, inc=1, device_id=sibling, device_id_type=pl.DeviceIdType.MESH
     )
+    routes = [
+        pltpu.make_async_copy(src, dst, r_loc.at[i])
+        for i, (src, dst) in enumerate(
+            ((index_in, index), (count_in, count), (gate_in, gate))
+        )
+    ]
+    for c in routes:
+        c.start()
     tok_copies = {}
     for k in far_first:
         tok_copies[k] = pltpu.make_async_copy(
@@ -412,6 +432,8 @@
     tgt_copy = pltpu.make_async_copy(target, TGT, g_loc)
     tgt_copy.start()
 
+    for c in routes:
+        c.wait()
     lane = lax.broadcasted_iota(jnp.int32, (slots, slots), 1)
     own_lane = lane == lax.broadcasted_iota(jnp.int32, (slots, slots), 0)
     slot_id = lax.broadcasted_iota(jnp.int32, (slots, 1), 0)
@@ -472,18 +494,28 @@
         remote(w, W.at[i, keep], w_send.at[i], w_recv.at[i], sibling)
         for i, w in enumerate((gw, uw, dw))
     ]
-    for k in far_first:
-        to_plane(
-            0, plane(k), lambda z, e: ROWS.at[slot_rows(e), cols(z)], R.at[slot_rows(me)]
-        )
+    outer = depth == planes - 1
+
+    def ordered(fn):
+        for ours, ks in ((outer, near_first), (jnp.logical_not(outer), far_first)):
+            @pl.when(ours)
+            def _():
+                for k in ks:
+                    fn(plane(k))
+
+    def send_tokens(z):
+        to_plane(0, z, lambda z, e: ROWS.at[slot_rows(e), cols(z)], R.at[slot_rows(me)])
+
+    if NEAR_TOKENS:
+        ordered(send_tokens)
+    else:
+        for k in far_first:
+            send_tokens(plane(k))
     with scope("trows"):
         tgt_copy.wait()
         for k in far_first:
             z = plane(k)
             TROWS[:, cols(z)] = dot(hot, TGT[:, cols(z)], NN).astype(BF16)
-            to_plane(
-                1, z, lambda z, e: TROWS.at[slot_rows(e), cols(z)], TR.at[slot_rows(me)]
-            )
     with scope("meta"):
         square = (per_group, per_group)
         eye = lax.broadcasted_iota(jnp.int32, square, 0) == lax.broadcasted_iota(
@@ -500,8 +532,6 @@
             step = pad if start == 0 else 128
             META[:, start:stop] = top
             META[:, start + step : stop + step] = (part - top.astype(F32)).astype(BF16)
-        for k in far_first:
-            to_plane(2, plane(k), lambda z, e: META.at[slot_rows(e)], MT.at[slot_rows(me)])
 
     with scope("w_wait"):
         for i in range(3):
@@ -591,14 +621,19 @@
                     mine, 2 * pad + 128 : 2 * pad + 129
                 ].astype(F32)
                 G[mine, :] = (wide - w * TR[mine, :].astype(F32)).astype(BF16)
-            HOWN[g] = dot(G[group_rows(z), :], W[2], NN)
+            for i in range(split):
+                HOWN[g * split + i] = dot(
+                    G[group_rows(z), :], W[2, :, i * hw : (i + 1) * hw], NN
+                )
             to_sibling(2, G.at[group_rows(z), give], GX.at[group_rows(z)])
 
     def backward(g):
         z = turn(g)
         rows = group_rows(z)
         with scope("bwd"):
-            hidden_grad = total(HOWN, HIN, g)
+            hidden_grad = jnp.concatenate(
+                [total(HOWN, HIN, g * split + i) for i in range(split)], axis=1
+            )
             for f in range(pieces):
                 both = OWN[g * pieces + f]
                 pre, up = both[:, :fw], both[:, fw:]
@@ -611,18 +646,18 @@
             RG[rows, :] = (
                 dot(GU[0, rows, :], W[0], NT) + dot(GU[1, rows, :], W[1], NT)
             ).astype(BF16)
-            to_plane(
-                3, z, lambda z, e: RG.at[slot_rows(z * experts + e)],
-                CB.at[slot_rows(me_e), cols(me_z)],
-            )
             for i in range(2):
                 to_sibling(3 + i, GU.at[i, rows], GUX.at[i, rows])
 
+    def send_rows(g):
+        to_plane(
+            3, turn(g), lambda z, e: RG.at[slot_rows(z * experts + e)],
+            CB.at[slot_rows(me_e), cols(me_z)],
+        )
+
     steps = planes * pieces
-    ready = LAG * depth
-    combined = pieces - 1 + ready + LAG_PLANE
-    started = pieces - 1 + LAG * (planes - 1) + LAG_PLANE
-    moved = started + LAG_BACK * depth
+    back_steps = planes * split
+    begin = pieces - 1 + LAG * (planes - 1) + LAG_PLANE
 
     def each(t, fn, last):
         @pl.when(jnp.logical_and(t >= 0, t < last))
@@ -630,41 +665,69 @@
             fn(t)
 
     def each_group(t, fn):
-        @pl.when(jnp.logical_and(jnp.logical_and(t >= 0, t < steps), t % pieces == 0))
-        def _():
-            fn(t // pieces)
+        fits = jnp.logical_and(t >= 0, t < back_steps)
+
+        @pl.when(jnp.logical_and(fits, t % split == 0))
+        def _():
+            fn(t // split)
 
     def grad(i, left, left_x, right, right_x, out):
-        GRADS[i] = (dot(left, right, TN) + dot(left_x, right_x, TN)) * factor
-        c = pltpu.make_async_copy(GRADS.at[i], out, o_loc.at[i])
-        c.start()
+        out[...] = (dot(left, right, TN) + dot(left_x, right_x, TN)) * factor
+
+    def send_targets(z):
+        to_plane(2, z, lambda z, e: META.at[slot_rows(e)], MT.at[slot_rows(me)])
+        to_plane(
+            1, z, lambda z, e: TROWS.at[slot_rows(e), cols(z)], TR.at[slot_rows(me)]
+        )
+
+    rank = jnp.maximum(planes // 2 - 1 - me_z, me_z - planes // 2)
+    target_at = TARGET_AT + TARGET_STEP * rank
+
+    def targets():
+        if NEAR_TARGETS:
+            ordered(send_targets)
+        else:
+            for k in far_first:
+                send_targets(plane(k))
+
+    @pl.when(target_at < 0)
+    def _():
+        targets()
 
     def tick(t, carry):
+        @pl.when(t == target_at)
+        def _():
+            targets()
+
         each(t, partial_sums, steps)
         for d in range(2):
             each(
                 t - LAG * dist[d],
                 functools.partial(move, OWN, IN, OUT, c_send, c_recv, d), steps,
             )
-        each(t - ready, forward, steps)
-        each_group(t - combined, slot_grads)
+        each(t - LAG * depth, forward, steps)
+        t = t - begin
+        each_group(t, slot_grads)
         for d in range(2):
-            each_group(
-                t - started - LAG_BACK * dist[d],
-                functools.partial(move, HOWN, HIN, HOUT, h_send, h_recv, d),
+            each(
+                t - LAG_BACK * dist[d],
+                functools.partial(move, HOWN, HIN, HOUT, h_send, h_recv, d), back_steps,
             )
-        each_group(t - moved, backward)
+        back = t - LAG_BACK * depth - (split - 1)
+        each_group(back, backward)
+        each_group(back - LAG_ROWS, send_rows)
         return carry
 
-    end = steps - pieces + pieces - 1 + (LAG + LAG_BACK) * (planes - 1) + LAG_PLANE + 1
-    middle = steps - pieces + pieces - 1 + LAG * (planes - 1) + LAG_PLANE + 1
+    middle = begin + back_steps + 1
     lax.fori_loop(0, middle, tick, 0)
     to_sibling(0, R.at[:, give], RX)
     with scope("dgrad"):
         take(x_recv.at[1], HX)
         take(x_recv.at[2], GX)
         grad(2, G[:, keep], GX[...], H[...], HX[...], dg_out)
-    lax.fori_loop(middle, end, tick, 0)
+    lax.fori_loop(
+        middle, begin + back_steps + LAG_BACK * (planes - 1) + LAG_ROWS + split, tick, 0
+    )
     with scope("xg"):
         take(x_recv.at[0], RX)
         take(x_recv.at[3], GUX.at[0])
@@ -676,8 +739,7 @@
         for k in far_first:
             take(a_recv.at[3, plane(k)], R.at[pl.ds(0, per_group)])
     with scope("tail"):
-        back = pltpu.make_async_copy(CB, cb_out, o_loc.at[3])
-        back.start()
+        cb_out[...] = CB[...]
         for c in sent_w:
             c.wait_send()
         others = pl.ds(0, (peers - 1) * slots)
@@ -691,16 +753,22 @@
                 take(h_send.at[d], HOUT.at[d])
         for i, buf in enumerate((RX, HX, GX, GUX.at[0], GUX.at[1])):
             take(x_send.at[i], buf)
-        for i, out in enumerate((gg_out, ug_out, dg_out)):
-            pltpu.make_async_copy(GRADS.at[i], out, o_loc.at[i]).wait()
-        back.wait()
-
-
-def finish(hot, cb, gg, ug, dg, tg_out, gg_out, ug_out, dg_out):
-    tg_out[...] = dot(hot[...], cb[...], TN).astype(BF16)
-    gg_out[:, 0, :] = gg[...]
-    ug_out[:, 0, :] = ug[...]
-    dg_out[:, 0, :] = dg[...]
+
+
+def finish(hot, cb, gg, ug, dg, tg_out, gg_out, ug_out, dg_out, TG, t_sem, g_sem):
+    copies = []
+    for i, (grad, out) in enumerate(((gg, gg_out), (ug, ug_out), (dg, dg_out))):
+        copies.append(pltpu.make_async_copy(grad, out.at[:, 0, :], g_sem.at[i]))
+        copies[-1].start()
+    parts = t_sem.shape[0]
+    step = TG.shape[0] // parts
+    for j in range(parts):
+        rows = slice(j * step, (j + 1) * step)
+        TG[rows, :] = dot(hot[:, rows], cb[...], TN).astype(BF16)
+        copies.append(pltpu.make_async_copy(TG.at[rows], tg_out.at[rows], t_sem.at[j]))
+        copies[-1].start()
+    for c in copies:
+        c.wait()
 
 
 def direct_scratch(planes, picked, count, width, half, ff):
@@ -738,7 +806,8 @@
     ]
 
 
-def chain_scratch(planes, experts, picked, count, width, half, ff, pieces):
+def chain_scratch(planes, experts, picked, count, width, half, ff, pieces, split):
+    slots = picked // experts
     chunk = CORES * half
     all_rows = planes * picked
     steps = planes * pieces
@@ -746,6 +815,10 @@
     table = 2 * (-(-picked // 128) * 128) + 256
     dma = pltpu.SemaphoreType.DMA
     return [
+        pltpu.VMEM((1, experts, 1, slots), jnp.int32),
+        pltpu.VMEM((1, experts), jnp.int32),
+        pltpu.VMEM((1, experts, 1, slots), F32),
+        dma((3,)),
         pltpu.VMEM((count, width), BF16),
         pltpu.VMEM((count, width), BF16),
         pltpu.VMEM((picked, width), BF16),
@@ -760,9 +833,9 @@
         pltpu.VMEM((steps, picked, 2 * fw), F32),
         pltpu.VMEM((2, steps, picked, 2 * fw), BF16),
         pltpu.VMEM((2, steps, picked, 2 * fw), BF16),
-        pltpu.VMEM((planes, picked, ff), F32),
-        pltpu.VMEM((2, planes, picked, ff), BF16),
-        pltpu.VMEM((2, planes, picked, ff), BF16),
+        pltpu.VMEM((planes * split, picked, ff // split), F32),
+        pltpu.VMEM((2, planes * split, picked, ff // split), BF16),
+        pltpu.VMEM((2, planes * split, picked, ff // split), BF16),
         pltpu.VMEM((all_rows, ff), BF16),
         pltpu.VMEM((2, all_rows, ff), BF16),
         pltpu.VMEM((all_rows, chunk), BF16),
@@ -771,11 +844,10 @@
         pltpu.VMEM((all_rows, half), BF16),
         pltpu.VMEM((all_rows, ff), BF16),
         pltpu.VMEM((2, all_rows, ff), BF16),
-        pltpu.VMEM((3, half, ff), F32),
         dma((planes,)), dma, dma((3,)), dma((3,)), dma((3,)),
         dma((4,)), dma((4, planes)), dma, dma((planes,)),
-        dma((2,)), dma((2, steps)), dma((2,)), dma((2, planes)),
-        dma((5,)), dma((5,)), dma((4,)),
+        dma((2,)), dma((2, steps)), dma((2,)), dma((2, planes * split)),
+        dma((5,)), dma((5,)),
     ]
 
 
@@ -798,15 +870,20 @@
     half, _, ff = gate_weight.shape
     picked = experts * slots
     factor = (groups * experts * slots) ** (-0.5)
-    pieces = max(n for n in range(1, PIECES + 1) if ff % (128 * n) == 0)
+    pieces, split = (
+        max(n for n in range(1, most + 1) if ff % (128 * n) == 0)
+        for most in (PIECES, BACK_PIECES)
+    )
     vmem = pl.BlockSpec(memory_space=pltpu.VMEM)
     anyw = pl.BlockSpec(memory_space=pl.ANY)
     grad = jax.ShapeDtypeStruct((half, ff), F32)
-    scratch = chain_scratch(planes, experts, picked, count, width, half, ff, pieces)
+    scratch = chain_scratch(planes, experts, picked, count, width, half, ff, pieces, split)
     body = functools.partial(chain_kernel, planes, experts, slots, factor, pieces)
-    if held_bytes(scratch) > VMEM_LIMIT * 3 // 4:
+    out, limit, small = vmem, CHAIN_LIMIT, anyw
+    if held_bytes(scratch) > CHAIN_LIMIT * 3 // 4:
         scratch = direct_scratch(planes, picked, count, width, half, ff)
         body = functools.partial(direct_kernel, planes, experts, slots, factor)
+        out, limit, small = anyw, VMEM_LIMIT, vmem
     came_back, hot, gate_gradient, up_gradient, down_gradient = pl.pallas_call(
         body,
         out_shape=(
@@ -814,36 +891,34 @@
             jax.ShapeDtypeStruct((picked, count), BF16),
             grad, grad, grad,
         ),
-        in_specs=[vmem] * 3 + [anyw] * 5,
-        out_specs=(anyw, vmem) + (anyw,) * 3,
+        in_specs=[small] * 3 + [anyw] * 5,
+        out_specs=(out, vmem, out, out, out),
         scratch_shapes=scratch,
         compiler_params=pltpu.CompilerParams(
-            collective_id=0, has_side_effects=True, vmem_limit_bytes=VMEM_LIMIT
+            collective_id=0, has_side_effects=True, vmem_limit_bytes=limit
         ),
         name="routed_layer",
     )(
-        route_index, route_count.reshape(1, experts), route_gate, tokens, target,
-        gate_weight.reshape(half, ff), up_weight.reshape(half, ff),
-        down_weight.reshape(half, ff),
+        *(
+            pltpu.with_memory_space_constraint(x, pltpu.MemorySpace.HBM)
+            for x in (
+                route_index, route_count.reshape(1, experts), route_gate, tokens, target, gate_weight.reshape(half, ff), up_weight.reshape(half, ff),
+                down_weight.reshape(half, ff),
+            )
+        ),
     )
-    steps = 2
-    part = pl.BlockSpec((half // steps, ff), lambda i: (i, 0))
-    part_out = pl.BlockSpec((half // steps, 1, ff), lambda i: (i, 0, 0))
+    parts = max(n for n in range(1, 9) if count % (128 * n) == 0)
     grad = jax.ShapeDtypeStruct((half, 1, ff), F32)
     return tuple(pl.pallas_call(
         finish,
-        grid=(steps,),
         out_shape=(jax.ShapeDtypeStruct((count, width), BF16), grad, grad, grad),
-        in_specs=[
-            pl.BlockSpec((picked, count // steps), lambda i: (0, i)),
-            pl.BlockSpec((picked, width), lambda i: (0, 0)),
-            part, part, part,
+        in_specs=[vmem] * 5,
+        out_specs=[anyw] * 4,
+        scratch_shapes=[
+            pltpu.VMEM((count, width), BF16),
+            pltpu.SemaphoreType.DMA((parts,)), pltpu.SemaphoreType.DMA((3,)),
         ],
-        out_specs=(
-            pl.BlockSpec((count // steps, width), lambda i: (i, 0)),
-            part_out, part_out, part_out,
-        ),
-        compiler_params=pltpu.CompilerParams(vmem_limit_bytes=VMEM_LIMIT),
+        compiler_params=pltpu.CompilerParams(vmem_limit_bytes=FINISH_LIMIT),
         name="finish",
     )(hot, came_back, gate_gradient, up_gradient, down_gradient))
 

time: 81.4 us -> 70.4 us (0.86)
  Pallas kernels: 80.1 us -> 69.5 us
    pallas_call x1, Pallas kernels: 75.5 us -> 67 us  [on_device(): pl.pallas_call(body, out_shape=(jax.ShapeDtypeStruct((picked, width), BF1...]
    pallas_call x1, Pallas kernels: 4.52 us -> 2.5 us  [on_device(): pl.pallas_call(finish, out_shape=(jax.ShapeDtypeStruct((count, width), BF...]
where the time goes in v2:
time: 70.4 us; the launch traced here: 70.2 us
  Pallas kernels  69.5 us (99%)
    pallas_call x1, Pallas kernels, on_device(): pl.pallas_call(body, out_shape=(jax.ShapeDtypeStruct((picked, width), BF1...  67 us
    pallas_call x1, Pallas kernels, on_device(): pl.pallas_call(finish, out_shape=(jax.ShapeDtypeStruct((count, width), BF...  2.5 us

profile of v2, /device:TPU:0, one launch (start us, length us, event | category | flops | bytes accessed | tf_op | source)
XLA Modules:
  0.0 70.2 jit_solution(17176009766301988019)
XLA Ops:
  0.6 67.0 %routed_layer.1 = (bf16[64,2048]{1,0:T(8,128)(2,1)S(1)}, bf16[64,768]{1,0:T(8,128)(2,1)S(1)}, f32[256,768]{1,0:T(8,128)S(1)}, f32[256,768]{1,0:T(8,128)S(1)}, f32[256,768]{1,0:T(8,128)S(1)}) custom-call(s32[1,4,1,16]{3,2,1,0:T(1,128)} %index_in.1, s32[1,4]{1,0:T(1,128)} %bitcast.7, f32[1,4,1,16]{3,2,1,0:T(1,128)} %gate_in.1, bf16[768,2048]{1,0:T(8,128)(2,1)} %tokens.1, ...), custom_call_target="tpu_custom_call" | custom-call | tf_op jit(solution)/shard_map/routed_layer/pallas_call | solution.py:887
  67.7 2.5 %finish.1 = (bf16[768,2048]{1,0:T(8,128)(2,1)}, f32[256,1,768]{2,1,0:T(1,128)}, f32[256,1,768]{2,1,0:T(1,128)}, f32[256,1,768]{2,1,0:T(1,128)}) custom-call(bf16[64,768]{1,0:T(8,128)(2,1)S(1)} %get-tuple-element.9.hot, bf16[64,2048]{1,0:T(8,128)(2,1)S(1)} %get-tuple-element.10.cb, f32[256,768]{1,0:T(8,128)S(1)} %get-tuple-element.11.gg, ...), custom_call_target="tpu_custom_call" | custom-call | tf_op jit(solution)/shard_map/finish/pallas_call | solution.py:912

commit v3 on v2

--- a/solution.py
+++ b/solution.py
@@ -14,15 +14,15 @@
 VMEM_LIMIT = 67000000
 CORES = 2
 PIECES = 3
-LAG = 3
-LAG_PLANE = 4
-LAG_BACK = 4
-LAG_ROWS = 0
 BACK_PIECES = 3
-TARGET_AT = -1
-TARGET_STEP = 0
-NEAR_TOKENS = False
-NEAR_TARGETS = False
+PARTS = 2
+LAG = 5
+LAG_PLANE = 6
+LAG_BACK = 6
+LAG_GRADS = 0
+LATE = True
+TURNS = (1, 0)
+OUTER_FIRST = True
 CHAIN_LIMIT = 44000000
 FINISH_LIMIT = 40000000
 
@@ -345,7 +345,7 @@
 
 
 def chain_kernel(
-    planes, experts, slots, factor, pieces,
+    planes, experts, slots, factor, pieces, parts,
     index_in, count_in, gate_in, tokens, target, gw, uw, dw,
     cb_out, hot_out, gg_out, ug_out, dg_out,
     index, count, gate, r_loc, TOK, TGT, ROWS, TROWS, META, MT, W, R, TR, G, EOG,
@@ -363,13 +363,13 @@
     chunk = CORES * half
     ff = gw.shape[1]
     fw = ff // pieces
-    split = HIN.shape[1] // planes
+    split = HIN.shape[1] // (planes * parts)
+    unit = per_group // parts
     hw = ff // split
     me = me_z * experts + me_e
     sibling = {"dp": me_z * CORES + (1 - core), "expert": me_e}
     ways = (1, -1)
     side = jnp.where(2 * me_z < planes, 1, -1)
-    near_first = list(range(1, planes)) + [0]
     far_first = sorted(range(1, planes), key=lambda k: abs(k - planes / 2)) + [0]
     dist = (me_z, planes - 1 - me_z)
     depth = jnp.maximum(dist[0], dist[1])
@@ -389,9 +389,14 @@
     def group_rows(z):
         return pl.ds(pl.multiple_of(z * per_group, per_group), per_group)
 
+    def unit_rows(n):
+        rows = turn(n // parts) * per_group + n % parts * unit
+        return pl.ds(pl.multiple_of(rows, unit), unit)
+
     def turn(g):
         if planes % 2:
             return g
+        g = planes - 1 - g if OUTER_FIRST else g
         return planes // 2 - 1 - g // 2 + (g % 2) * (2 * (g // 2) + 1)
 
     barrier = pltpu.get_barrier_semaphore()
@@ -494,23 +499,10 @@
         remote(w, W.at[i, keep], w_send.at[i], w_recv.at[i], sibling)
         for i, w in enumerate((gw, uw, dw))
     ]
-    outer = depth == planes - 1
-
-    def ordered(fn):
-        for ours, ks in ((outer, near_first), (jnp.logical_not(outer), far_first)):
-            @pl.when(ours)
-            def _():
-                for k in ks:
-                    fn(plane(k))
-
-    def send_tokens(z):
-        to_plane(0, z, lambda z, e: ROWS.at[slot_rows(e), cols(z)], R.at[slot_rows(me)])
-
-    if NEAR_TOKENS:
-        ordered(send_tokens)
-    else:
-        for k in far_first:
-            send_tokens(plane(k))
+    for k in far_first:
+        to_plane(
+            0, plane(k), lambda z, e: ROWS.at[slot_rows(e), cols(z)], R.at[slot_rows(me)]
+        )
     with scope("trows"):
         tgt_copy.wait()
         for k in far_first:
@@ -541,22 +533,16 @@
     def piece(f):
         return pl.ds(pl.multiple_of(f * fw, fw), fw)
 
-    def group_of(c):
-        return turn(c // pieces)
-
-    def rows_in(z):
-        take(a_recv.at[0, z], R.at[pl.ds(0, per_group)])
-
     def partial_sums(c):
-        z, f = group_of(c), c % pieces
-
-        @pl.when(f == 0)
+        n, f = c // pieces, c % pieces
+
+        @pl.when(c % (pieces * parts) == 0)
         def _():
             with scope("x_wait"):
-                rows_in(z)
+                take(a_recv.at[0, turn(n // parts)], R.at[pl.ds(0, per_group)])
 
         with scope("own"):
-            rows = R[group_rows(z), :]
+            rows = R[unit_rows(n), :]
             for i in range(2):
                 OWN[c, :, i * fw : (i + 1) * fw] = dot(rows, W[i, :, piece(f)], NN)
 
@@ -581,39 +567,43 @@
         remote(src, dst, x_send.at[i], x_recv.at[i], sibling)
 
     def forward(c):
-        z, f = group_of(c), c % pieces
+        n, f = c // pieces, c % pieces
+        rows = unit_rows(n)
         with scope("fwd"):
             both = total(OWN, IN, c)
             OWN[c] = both
             pre, up = both[:, :fw], both[:, fw:]
-            H[group_rows(z), piece(f)] = (pre * jax.nn.sigmoid(pre) * up).astype(BF16)
+            H[rows, piece(f)] = (pre * jax.nn.sigmoid(pre) * up).astype(BF16)
 
         @pl.when(f == pieces - 1)
         def _():
             with scope("eo"):
-                EOG[z, me_e] = dot(H[group_rows(z), :], W[2], NT).astype(BF16)
+                EOG[me_e, rows, :] = dot(H[rows, :], W[2], NT).astype(BF16)
+                outs = EOG.at[me_e, rows]
 
                 def send(j, carry):
                     remote(
-                        EOG.at[z, me_e], EOG.at[z, me_e], e_send, e_recv.at[z],
-                        at(me_z, (me_e + j) % experts),
+                        outs, outs, e_send, e_recv.at[n], at(me_z, (me_e + j) % experts)
                     )
                     return carry
 
                 lax.fori_loop(1, experts, send, 0)
-                to_sibling(1, H.at[group_rows(z)], HX.at[group_rows(z)])
-
-    def slot_grads(g):
-        z = turn(g)
+                to_sibling(1, H.at[rows], HX.at[rows])
+
+    def slot_grads(n):
+        z = turn(n // parts)
+        rows = unit_rows(n)
         with scope("eo_wait"):
-            take(e_recv.at[z], EOG.at[z, pl.ds(0, experts - 1)])
-            take(a_recv.at[1, z], TR.at[pl.ds(0, per_group)])
-            take(a_recv.at[2, z], MT.at[pl.ds(0, per_group)])
+            take(e_recv.at[n], EOG.at[pl.ds(0, experts - 1), pl.ds(0, unit)])
+
+            @pl.when(n % parts == 0)
+            def _():
+                take(a_recv.at[1, z], TR.at[pl.ds(0, per_group)])
+                take(a_recv.at[2, z], MT.at[pl.ds(0, per_group)])
         with scope("comb"):
-            for s in range(experts):
-                its = slice(s * slots, (s + 1) * slots)
-                mine = slot_rows(z * experts + s)
-                outs = jnp.concatenate([EOG[z, e, its, :] for e in range(experts)], axis=0)
+            for s in range(experts // parts):
+                mine = slot_rows(z * experts + n % parts * (experts // parts) + s)
+                outs = jnp.concatenate([EOG[e, mine, :] for e in range(experts)], axis=0)
                 wide = dot(MT[mine, 0:per_group], outs, NN) + dot(
                     MT[mine, pad : pad + per_group], outs, NN
                 )
@@ -622,20 +612,17 @@
                 ].astype(F32)
                 G[mine, :] = (wide - w * TR[mine, :].astype(F32)).astype(BF16)
             for i in range(split):
-                HOWN[g * split + i] = dot(
-                    G[group_rows(z), :], W[2, :, i * hw : (i + 1) * hw], NN
-                )
-            to_sibling(2, G.at[group_rows(z), give], GX.at[group_rows(z)])
-
-    def backward(g):
-        z = turn(g)
-        rows = group_rows(z)
+                HOWN[n * split + i] = dot(G[rows, :], W[2, :, i * hw : (i + 1) * hw], NN)
+            to_sibling(2, G.at[rows, give], GX.at[rows])
+
+    def backward(n):
+        rows = unit_rows(n)
         with scope("bwd"):
             hidden_grad = jnp.concatenate(
-                [total(HOWN, HIN, g * split + i) for i in range(split)], axis=1
+                [total(HOWN, HIN, n * split + i) for i in range(split)], axis=1
             )
             for f in range(pieces):
-                both = OWN[g * pieces + f]
+                both = OWN[n * pieces + f]
                 pre, up = both[:, :fw], both[:, fw:]
                 grad = hidden_grad[:, f * fw : (f + 1) * fw]
                 sigma = jax.nn.sigmoid(pre)
@@ -646,18 +633,35 @@
             RG[rows, :] = (
                 dot(GU[0, rows, :], W[0], NT) + dot(GU[1, rows, :], W[1], NT)
             ).astype(BF16)
+            send_rows(n)
             for i in range(2):
                 to_sibling(3 + i, GU.at[i, rows], GUX.at[i, rows])
 
-    def send_rows(g):
-        to_plane(
-            3, turn(g), lambda z, e: RG.at[slot_rows(z * experts + e)],
-            CB.at[slot_rows(me_e), cols(me_z)],
-        )
-
-    steps = planes * pieces
-    back_steps = planes * split
+    def send_rows(n):
+        z, share = turn(n // parts), experts // parts
+        land = CB.at[slot_rows(me_e), cols(me_z)]
+
+        def send(j, carry):
+            e = n % parts * share + j
+            rows = RG.at[slot_rows(z * experts + e)]
+            here = jnp.logical_and(z == me_z, e == me_e)
+
+            @pl.when(here)
+            def _():
+                pltpu.make_async_copy(rows, land, a_recv.at[3, me_z]).start()
+
+            @pl.when(jnp.logical_not(here))
+            def _():
+                remote(rows, land, a_send.at[3], a_recv.at[3, me_z], at(z, e))
+
+            return carry
+
+        lax.fori_loop(0, share, send, 0)
+
+    steps = planes * parts * pieces
+    back_steps = planes * parts * split
     begin = pieces - 1 + LAG * (planes - 1) + LAG_PLANE
+    begin += max(0, pieces - split) * (planes * parts - 1)
 
     def each(t, fn, last):
         @pl.when(jnp.logical_and(t >= 0, t < last))
@@ -680,27 +684,12 @@
             1, z, lambda z, e: TROWS.at[slot_rows(e), cols(z)], TR.at[slot_rows(me)]
         )
 
-    rank = jnp.maximum(planes // 2 - 1 - me_z, me_z - planes // 2)
-    target_at = TARGET_AT + TARGET_STEP * rank
-
-    def targets():
-        if NEAR_TARGETS:
-            ordered(send_targets)
-        else:
-            for k in far_first:
-                send_targets(plane(k))
-
-    @pl.when(target_at < 0)
-    def _():
-        targets()
+    for k in far_first:
+        send_targets(plane(k))
 
     def tick(t, carry):
-        @pl.when(t == target_at)
-        def _():
-            targets()
-
         each(t, partial_sums, steps)
-        for d in range(2):
+        for d in TURNS:
             each(
                 t - LAG * dist[d],
                 functools.partial(move, OWN, IN, OUT, c_send, c_recv, d), steps,
@@ -708,14 +697,13 @@
         each(t - LAG * depth, forward, steps)
         t = t - begin
         each_group(t, slot_grads)
-        for d in range(2):
+        for d in TURNS:
             each(
                 t - LAG_BACK * dist[d],
                 functools.partial(move, HOWN, HIN, HOUT, h_send, h_recv, d), back_steps,
             )
-        back = t - LAG_BACK * depth - (split - 1)
+        back = t - LAG_BACK * (planes - 1 if LATE else depth) - (split - 1) - LAG_GRADS
         each_group(back, backward)
-        each_group(back - LAG_ROWS, send_rows)
         return carry
 
     middle = begin + back_steps + 1
@@ -726,7 +714,7 @@
         take(x_recv.at[2], GX)
         grad(2, G[:, keep], GX[...], H[...], HX[...], dg_out)
     lax.fori_loop(
-        middle, begin + back_steps + LAG_BACK * (planes - 1) + LAG_ROWS + split, tick, 0
+        middle, begin + back_steps + LAG_BACK * (planes - 1) + LAG_GRADS + split, tick, 0
     )
     with scope("xg"):
         take(x_recv.at[0], RX)
@@ -745,7 +733,7 @@
         others = pl.ds(0, (peers - 1) * slots)
         for i, buf in enumerate((R, TR, MT, RG)):
             take(a_send.at[i], buf.at[others])
-        take(e_send, EOG.at[:, pl.ds(0, experts - 1)])
+        take(e_send, EOG.at[pl.ds(0, experts - 1)])
         for d in range(2):
             @pl.when(dist[d] < planes - 1)
             def _():
@@ -806,11 +794,13 @@
     ]
 
 
-def chain_scratch(planes, experts, picked, count, width, half, ff, pieces, split):
+def chain_scratch(planes, experts, picked, count, width, half, ff, pieces, split, parts):
     slots = picked // experts
     chunk = CORES * half
     all_rows = planes * picked
-    steps = planes * pieces
+    steps = planes * parts * pieces
+    back_steps = planes * parts * split
+    unit = picked // parts
     fw = ff // pieces
     table = 2 * (-(-picked // 128) * 128) + 256
     dma = pltpu.SemaphoreType.DMA
@@ -829,13 +819,13 @@
         pltpu.VMEM((all_rows, chunk), BF16),
         pltpu.VMEM((all_rows, chunk), BF16),
         pltpu.VMEM((all_rows, chunk), BF16),
-        pltpu.VMEM((planes, experts, picked, chunk), BF16),
-        pltpu.VMEM((steps, picked, 2 * fw), F32),
-        pltpu.VMEM((2, steps, picked, 2 * fw), BF16),
-        pltpu.VMEM((2, steps, picked, 2 * fw), BF16),
-        pltpu.VMEM((planes * split, picked, ff // split), F32),
-        pltpu.VMEM((2, planes * split, picked, ff // split), BF16),
-        pltpu.VMEM((2, planes * split, picked, ff // split), BF16),
+        pltpu.VMEM((experts, all_rows, chunk), BF16),
+        pltpu.VMEM((steps, unit, 2 * fw), F32),
+        pltpu.VMEM((2, steps, unit, 2 * fw), BF16),
+        pltpu.VMEM((2, steps, unit, 2 * fw), BF16),
+        pltpu.VMEM((back_steps, unit, ff // split), F32),
+        pltpu.VMEM((2, back_steps, unit, ff // split), BF16),
+        pltpu.VMEM((2, back_steps, unit, ff // split), BF16),
         pltpu.VMEM((all_rows, ff), BF16),
         pltpu.VMEM((2, all_rows, ff), BF16),
         pltpu.VMEM((all_rows, chunk), BF16),
@@ -845,8 +835,8 @@
         pltpu.VMEM((all_rows, ff), BF16),
         pltpu.VMEM((2, all_rows, ff), BF16),
         dma((planes,)), dma, dma((3,)), dma((3,)), dma((3,)),
-        dma((4,)), dma((4, planes)), dma, dma((planes,)),
-        dma((2,)), dma((2, steps)), dma((2,)), dma((2, planes * split)),
+        dma((4,)), dma((4, planes)), dma, dma((planes * parts,)),
+        dma((2,)), dma((2, steps)), dma((2,)), dma((2, back_steps)),
         dma((5,)), dma((5,)),
     ]
 
@@ -877,8 +867,11 @@
     vmem = pl.BlockSpec(memory_space=pltpu.VMEM)
     anyw = pl.BlockSpec(memory_space=pl.ANY)
     grad = jax.ShapeDtypeStruct((half, ff), F32)
-    scratch = chain_scratch(planes, experts, picked, count, width, half, ff, pieces, split)
-    body = functools.partial(chain_kernel, planes, experts, slots, factor, pieces)
+    parts = PARTS if experts % PARTS == 0 else 1
+    scratch = chain_scratch(
+        planes, experts, picked, count, width, half, ff, pieces, split, parts
+    )
+    body = functools.partial(chain_kernel, planes, experts, slots, factor, pieces, parts)
     out, limit, small = vmem, CHAIN_LIMIT, anyw
     if held_bytes(scratch) > CHAIN_LIMIT * 3 // 4:
         scratch = direct_scratch(planes, picked, count, width, half, ff)
@@ -907,7 +900,7 @@
             )
         ),
     )
-    parts = max(n for n in range(1, 9) if count % (128 * n) == 0)
+    blocks = max(n for n in range(1, 9) if count % (128 * n) == 0)
     grad = jax.ShapeDtypeStruct((half, 1, ff), F32)
     return tuple(pl.pallas_call(
         finish,
@@ -916,7 +909,7 @@
         out_specs=[anyw] * 4,
         scratch_shapes=[
             pltpu.VMEM((count, width), BF16),
-            pltpu.SemaphoreType.DMA((parts,)), pltpu.SemaphoreType.DMA((3,)),
+            pltpu.SemaphoreType.DMA((blocks,)), pltpu.SemaphoreType.DMA((3,)),
         ],
         compiler_params=pltpu.CompilerParams(vmem_limit_bytes=FINISH_LIMIT),
         name="finish",

time: 70.4 us -> 68 us (0.966)
  Pallas kernels: 69.5 us -> 67 us
    pallas_call x1, Pallas kernels: 67 us -> 64.5 us  [on_device(): pl.pallas_call(body, out_shape=(jax.ShapeDtypeStruct((picked, width), BF1...]
where the time goes in v3:
time: 68 us; the launch traced here: 67.7 us
  Pallas kernels  67 us (99%)
    pallas_call x1, Pallas kernels, on_device(): pl.pallas_call(body, out_shape=(jax.ShapeDtypeStruct((picked, width), BF1...  64.5 us
    pallas_call x1, Pallas kernels, on_device(): pl.pallas_call(finish, out_shape=(jax.ShapeDtypeStruct((count, width), BF...  2.5 us

profile of v3, /device:TPU:0, one launch (start us, length us, event | category | flops | bytes accessed | tf_op | source)
XLA Modules:
  0.0 67.7 jit_solution(13957340210867190447)
XLA Ops:
  0.6 64.5 %routed_layer.1 = (bf16[64,2048]{1,0:T(8,128)(2,1)S(1)}, bf16[64,768]{1,0:T(8,128)(2,1)S(1)}, f32[256,768]{1,0:T(8,128)S(1)}, f32[256,768]{1,0:T(8,128)S(1)}, f32[256,768]{1,0:T(8,128)S(1)}) custom-call(s32[1,4,1,16]{3,2,1,0:T(1,128)} %index_in.1, s32[1,4]{1,0:T(1,128)} %bitcast.7, f32[1,4,1,16]{3,2,1,0:T(1,128)} %gate_in.1, bf16[768,2048]{1,0:T(8,128)(2,1)} %tokens.1, ...), custom_call_target="tpu_custom_call" | custom-call | tf_op jit(solution)/shard_map/routed_layer/pallas_call | solution.py:880
  65.2 2.5 %finish.1 = (bf16[768,2048]{1,0:T(8,128)(2,1)}, f32[256,1,768]{2,1,0:T(1,128)}, f32[256,1,768]{2,1,0:T(1,128)}, f32[256,1,768]{2,1,0:T(1,128)}) custom-call(bf16[64,768]{1,0:T(8,128)(2,1)S(1)} %get-tuple-element.9.hot, bf16[64,2048]{1,0:T(8,128)(2,1)S(1)} %get-tuple-element.10.cb, f32[256,768]{1,0:T(8,128)S(1)} %get-tuple-element.11.gg, ...), custom_call_target="tpu_custom_call" | custom-call | tf_op jit(solution)/shard_map/finish/pallas_call | solution.py:905

commit v4 on v3

--- a/solution.py
+++ b/solution.py
@@ -514,16 +514,12 @@
             jnp.int32, square, 1
         )
         wrow = jnp.sum(jnp.where(eye, wcol, 0.0), axis=0, keepdims=True)
-        mix = wcol * dot(hot, hot, NT) * wrow
-        pad = (META.shape[1] - 256) // 2
-        META[...] = jnp.zeros(META.shape, BF16)
-        for part, start, stop in (
-            (mix, 0, per_group), (jnp.broadcast_to(wcol, (per_group, 128)), 2 * pad, 2 * pad + 128)
-        ):
-            top = part.astype(BF16)
-            step = pad if start == 0 else 128
-            META[:, start:stop] = top
-            META[:, start + step : stop + step] = (part - top.astype(F32)).astype(BF16)
+        mix = dot(hot, hot, NT) * wrow
+        top = mix.astype(BF16)
+        if META.shape[1] > 2 * per_group:
+            META[...] = jnp.zeros(META.shape, BF16)
+        META[:, 0:per_group] = top
+        META[:, per_group : 2 * per_group] = (mix - top.astype(F32)).astype(BF16)
 
     with scope("w_wait"):
         for i in range(3):
@@ -590,6 +586,12 @@
                 lax.fori_loop(1, experts, send, 0)
                 to_sibling(1, H.at[rows], HX.at[rows])
 
+    spread = (slots, 2 * per_group)
+    own_slot = (
+        lax.broadcasted_iota(jnp.int32, spread, 1) % per_group
+        == lax.broadcasted_iota(jnp.int32, spread, 0) + me_e * slots
+    )
+
     def slot_grads(n):
         z = turn(n // parts)
         rows = unit_rows(n)
@@ -603,14 +605,13 @@
         with scope("comb"):
             for s in range(experts // parts):
                 mine = slot_rows(z * experts + n % parts * (experts // parts) + s)
-                outs = jnp.concatenate([EOG[e, mine, :] for e in range(experts)], axis=0)
-                wide = dot(MT[mine, 0:per_group], outs, NN) + dot(
-                    MT[mine, pad : pad + per_group], outs, NN
+                outs = [EOG[e, mine, :] for e in range(experts)]
+                table = MT[mine, 0 : 2 * per_group]
+                wide = dot(table, jnp.concatenate(outs + outs, axis=0), NN)
+                w = jnp.sum(
+                    jnp.where(own_slot, table.astype(F32), 0.0), axis=1, keepdims=True
                 )
-                w = MT[mine, 2 * pad : 2 * pad + 1].astype(F32) + MT[
-                    mine, 2 * pad + 128 : 2 * pad + 129
-                ].astype(F32)
-                G[mine, :] = (wide - w * TR[mine, :].astype(F32)).astype(BF16)
+                G[mine, :] = (w * (wide - TR[mine, :].astype(F32))).astype(BF16)
             for i in range(split):
                 HOWN[n * split + i] = dot(G[rows, :], W[2, :, i * hw : (i + 1) * hw], NN)
             to_sibling(2, G.at[rows, give], GX.at[rows])
@@ -802,7 +803,7 @@
     back_steps = planes * parts * split
     unit = picked // parts
     fw = ff // pieces
-    table = 2 * (-(-picked // 128) * 128) + 256
+    table = -(-2 * picked // 128) * 128
     dma = pltpu.SemaphoreType.DMA
     return [
         pltpu.VMEM((1, experts, 1, slots), jnp.int32),

time: 68 us -> 64.7 us (0.951)
  Pallas kernels: 67 us -> 63.9 us
    pallas_call x1, Pallas kernels: 64.5 us -> 61.4 us  [on_device(): pl.pallas_call(body, out_shape=(jax.ShapeDtypeStruct((picked, width), BF1...]
where the time goes in v4:
time: 64.7 us; the launch traced here: 64.5 us
  Pallas kernels  63.9 us (99%)
    pallas_call x1, Pallas kernels, on_device(): pl.pallas_call(body, out_shape=(jax.ShapeDtypeStruct((picked, width), BF1...  61.4 us
    pallas_call x1, Pallas kernels, on_device(): pl.pallas_call(finish, out_shape=(jax.ShapeDtypeStruct((count, width), BF...  2.5 us

profile of v4, /device:TPU:0, one launch (start us, length us, event | category | flops | bytes accessed | tf_op | source)
XLA Modules:
  0.0 64.5 jit_solution(7231110083080082335)
XLA Ops:
  0.6 61.4 %routed_layer.1 = (bf16[64,2048]{1,0:T(8,128)(2,1)S(1)}, bf16[64,768]{1,0:T(8,128)(2,1)S(1)}, f32[256,768]{1,0:T(8,128)S(1)}, f32[256,768]{1,0:T(8,128)S(1)}, f32[256,768]{1,0:T(8,128)S(1)}) custom-call(s32[1,4,1,16]{3,2,1,0:T(1,128)} %index_in.1, s32[1,4]{1,0:T(1,128)} %bitcast.7, f32[1,4,1,16]{3,2,1,0:T(1,128)} %gate_in.1, bf16[768,2048]{1,0:T(8,128)(2,1)} %tokens.1, ...), custom_call_target="tpu_custom_call" | custom-call | tf_op jit(solution)/shard_map/routed_layer/pallas_call | solution.py:881
  62.0 2.5 %finish.1 = (bf16[768,2048]{1,0:T(8,128)(2,1)}, f32[256,1,768]{2,1,0:T(1,128)}, f32[256,1,768]{2,1,0:T(1,128)}, f32[256,1,768]{2,1,0:T(1,128)}) custom-call(bf16[64,768]{1,0:T(8,128)(2,1)S(1)} %get-tuple-element.9.hot, bf16[64,2048]{1,0:T(8,128)(2,1)S(1)} %get-tuple-element.10.cb, f32[256,768]{1,0:T(8,128)S(1)} %get-tuple-element.11.gg, ...), custom_call_target="tpu_custom_call" | custom-call | tf_op jit(solution)/shard_map/finish/pallas_call | solution.py:906

commit v5 on v4

--- a/solution.py
+++ b/solution.py
@@ -20,9 +20,9 @@
 LAG_PLANE = 6
 LAG_BACK = 6
 LAG_GRADS = 0
-LATE = True
+LATE = False
 TURNS = (1, 0)
-OUTER_FIRST = True
+OUTER_FIRST = False
 CHAIN_LIMIT = 44000000
 FINISH_LIMIT = 40000000
 
@@ -348,7 +348,7 @@
     planes, experts, slots, factor, pieces, parts,
     index_in, count_in, gate_in, tokens, target, gw, uw, dw,
     cb_out, hot_out, gg_out, ug_out, dg_out,
-    index, count, gate, r_loc, TOK, TGT, ROWS, TROWS, META, MT, W, R, TR, G, EOG,
+    index, count, gate, r_loc, TOK, TGT, ROWS, TROWS, META, MT, W, WT, R, TR, G, EOG,
     OWN, IN, OUT, HOWN, HIN, HOUT, H, GU, RG, CB, RX, GX, HX, GUX,
     t_loc, g_loc, w_loc, w_send, w_recv, a_send, a_recv, e_send, e_recv,
     c_send, c_recv, h_send, h_recv, x_send, x_recv,
@@ -525,6 +525,9 @@
         for i in range(3):
             locals_w[i].wait()
             sent_w[i].wait_recv()
+    with scope("wt"):
+        for i in range(3):
+            WT[i] = W[i].T
 
     def piece(f):
         return pl.ds(pl.multiple_of(f * fw, fw), fw)
@@ -574,7 +577,7 @@
         @pl.when(f == pieces - 1)
         def _():
             with scope("eo"):
-                EOG[me_e, rows, :] = dot(H[rows, :], W[2], NT).astype(BF16)
+                EOG[me_e, rows, :] = dot(H[rows, :], WT[2], NN).astype(BF16)
                 outs = EOG.at[me_e, rows]
 
                 def send(j, carry):
@@ -632,7 +635,7 @@
                 ).astype(BF16)
                 GU[1, rows, f * fw : (f + 1) * fw] = (grad * (pre * sigma)).astype(BF16)
             RG[rows, :] = (
-                dot(GU[0, rows, :], W[0], NT) + dot(GU[1, rows, :], W[1], NT)
+                dot(GU[0, rows, :], WT[0], NN) + dot(GU[1, rows, :], WT[1], NN)
             ).astype(BF16)
             send_rows(n)
             for i in range(2):
@@ -817,6 +820,7 @@
         pltpu.VMEM((picked, table), BF16),
         pltpu.VMEM((all_rows, table), BF16),
         pltpu.VMEM((3, chunk, ff), BF16),
+        pltpu.VMEM((3, ff, chunk), BF16),
         pltpu.VMEM((all_rows, chunk), BF16),
         pltpu.VMEM((all_rows, chunk), BF16),
         pltpu.VMEM((all_rows, chunk), BF16),

time: 64.7 us -> 62.8 us (0.971)
  Pallas kernels: 63.9 us -> 61.9 us
    pallas_call x1, Pallas kernels: 61.4 us -> 59.4 us  [on_device(): pl.pallas_call(body, out_shape=(jax.ShapeDtypeStruct((picked, width), BF1...]
where the time goes in v5:
time: 62.8 us; the launch traced here: 62.6 us
  Pallas kernels  61.9 us (99%)
  between operations  0.64 us (1%)
    pallas_call x1, Pallas kernels, on_device(): pl.pallas_call(body, out_shape=(jax.ShapeDtypeStruct((picked, width), BF1...  59.4 us
    pallas_call x1, Pallas kernels, on_device(): pl.pallas_call(finish, out_shape=(jax.ShapeDtypeStruct((count, width), BF...  2.5 us

profile of v5, /device:TPU:0, one launch (start us, length us, event | category | flops | bytes accessed | tf_op | source)
XLA Modules:
  0.0 62.6 jit_solution(16922287009952994725)
XLA Ops:
  0.6 59.4 %routed_layer.1 = (bf16[64,2048]{1,0:T(8,128)(2,1)S(1)}, bf16[64,768]{1,0:T(8,128)(2,1)S(1)}, f32[256,768]{1,0:T(8,128)S(1)}, f32[256,768]{1,0:T(8,128)S(1)}, f32[256,768]{1,0:T(8,128)S(1)}) custom-call(s32[1,4,1,16]{3,2,1,0:T(1,128)} %index_in.1, s32[1,4]{1,0:T(1,128)} %bitcast.7, f32[1,4,1,16]{3,2,1,0:T(1,128)} %gate_in.1, bf16[768,2048]{1,0:T(8,128)(2,1)} %tokens.1, ...), custom_call_target="tpu_custom_call" | custom-call | tf_op jit(solution)/shard_map/routed_layer/pallas_call | solution.py:885
  60.1 2.5 %finish.1 = (bf16[768,2048]{1,0:T(8,128)(2,1)}, f32[256,1,768]{2,1,0:T(1,128)}, f32[256,1,768]{2,1,0:T(1,128)}, f32[256,1,768]{2,1,0:T(1,128)}) custom-call(bf16[64,768]{1,0:T(8,128)(2,1)S(1)} %get-tuple-element.9.hot, bf16[64,2048]{1,0:T(8,128)(2,1)S(1)} %get-tuple-element.10.cb, f32[256,768]{1,0:T(8,128)S(1)} %get-tuple-element.11.gg, ...), custom_call_target="tpu_custom_call" | custom-call | tf_op jit(solution)/shard_map/finish/pallas_call | solution.py:910

commit v6 on v5

--- a/solution.py
+++ b/solution.py
@@ -18,7 +18,7 @@
 PARTS = 2
 LAG = 5
 LAG_PLANE = 6
-LAG_BACK = 6
+LAG_BACK = 7
 LAG_GRADS = 0
 LATE = False
 TURNS = (1, 0)

time: 62.8 us -> 62.8 us (level)
  no operation moved by 1% of the time
where the time goes in v6:
time: 62.8 us; the launch traced here: 62.7 us
  Pallas kernels  62 us (99%)
  between operations  0.64 us (1%)
    pallas_call x1, Pallas kernels, on_device(): pl.pallas_call(body, out_shape=(jax.ShapeDtypeStruct((picked, width), BF1...  59.5 us
    pallas_call x1, Pallas kernels, on_device(): pl.pallas_call(finish, out_shape=(jax.ShapeDtypeStruct((count, width), BF...  2.5 us

profile of v6, /device:TPU:0, one launch (start us, length us, event | category | flops | bytes accessed | tf_op | source)
XLA Modules:
  0.0 62.7 jit_solution(10145700799277981960)
XLA Ops:
  0.6 59.5 %routed_layer.1 = (bf16[64,2048]{1,0:T(8,128)(2,1)S(1)}, bf16[64,768]{1,0:T(8,128)(2,1)S(1)}, f32[256,768]{1,0:T(8,128)S(1)}, f32[256,768]{1,0:T(8,128)S(1)}, f32[256,768]{1,0:T(8,128)S(1)}) custom-call(s32[1,4,1,16]{3,2,1,0:T(1,128)} %index_in.1, s32[1,4]{1,0:T(1,128)} %bitcast.7, f32[1,4,1,16]{3,2,1,0:T(1,128)} %gate_in.1, bf16[768,2048]{1,0:T(8,128)(2,1)} %tokens.1, ...), custom_call_target="tpu_custom_call" | custom-call | tf_op jit(solution)/shard_map/routed_layer/pallas_call | solution.py:885
  60.2 2.5 %finish.1 = (bf16[768,2048]{1,0:T(8,128)(2,1)}, f32[256,1,768]{2,1,0:T(1,128)}, f32[256,1,768]{2,1,0:T(1,128)}, f32[256,1,768]{2,1,0:T(1,128)}) custom-call(bf16[64,768]{1,0:T(8,128)(2,1)S(1)} %get-tuple-element.9.hot, bf16[64,2048]{1,0:T(8,128)(2,1)S(1)} %get-tuple-element.10.cb, f32[256,768]{1,0:T(8,128)S(1)} %get-tuple-element.11.gg, ...), custom_call_target="tpu_custom_call" | custom-call | tf_op jit(solution)/shard_map/finish/pallas_call | solution.py:910
